TPU v7x, 512 devices: a whole 4x4x16 slice. The times are simulated.
512 devices in a mesh: seq: 32 (over z, core), head: 16 (over x, y).
Axes of the slice: x: 4, y: 4, z: 16, core: 2. Of those that a mesh axis runs over, the one named last changes fastest.
Arguments:
- queries: bfloat16 [32768, 16, 128], P(('seq', 'head')), may hold values from -6 to 6
- keys: bfloat16 [32768, 16, 128], P(('seq', 'head')), may hold values from -6 to 6
- values: bfloat16 [32768, 16, 128], P(('seq', 'head')), may hold values from -6 to 6
- log_decay: bfloat16 [32768, 16], P(('seq', 'head')), may hold values from -1 to 0
- beta: bfloat16 [32768, 16], P(('seq', 'head')), may hold values from 0.0099 to 0.6
- norm_gain: float32 [128], replicated, may hold values from 0.25 to 1.75
Outputs:
- normed_core: bfloat16 [32768, 16, 128], P(('seq', 'head'))
All inputs are finite; a program needn't handle non-finite values.
Results may differ from a plain program's by a relative error of at most 0.013.
Values may be sent and summed in bfloat16 or wider, within the bound.
No kernel may reach another device: no remote copies, remote signals or barrier semaphores. Data moves between devices by JAX's collectives and lax.ppermute only.
A program may use at most 64 MiB of HBM per device.

v0:
```python
import jax
import jax.numpy as jnp
from jax import lax
from jax.sharding import PartitionSpec as P

GROUP = 64


HIGH = lax.Precision.HIGHEST


def prefix_2(value, axis, join, neutral):
    count, mine = (lax.axis_size(axis), lax.axis_index(axis))
    pieces = jax.tree.map(lambda part: lax.all_gather(part, axis), value)
    total = jax.tree.map(
        lambda part, zero: jnp.full_like(part, 0) + jnp.asarray(zero, part.dtype), value, neutral
    )

    def turn(position, total):
        longer = join(total, jax.tree.map(lambda part: part[position], pieces))
        return jax.tree.map(lambda new, old: jnp.where(position < mine, new, old), longer, total)

    return lax.fori_loop(0, count - 1, turn, total)


def unit_rows(tensor):
    tensor = tensor.astype(jnp.float32)
    return tensor * lax.rsqrt(jnp.sum(tensor * tensor, axis=-1, keepdims=True) + 1e-06)


def multiply(left, right):
    return jnp.einsum("...ij,...jk->...ik", left, right, precision=HIGH)


def compose(earlier, later):
    return (multiply(later[0], earlier[0]), multiply(later[0], earlier[1]) + later[1])


def grouped(tensor):
    token_count, head_count, head_width = tensor.shape
    return tensor.reshape(token_count // GROUP, GROUP, head_count, head_width).transpose(2, 0, 1, 3)


def grouped_gate(tensor):
    token_count, head_count = tensor.shape
    return (
        tensor.astype(jnp.float32)
        .reshape(token_count // GROUP, GROUP, head_count)
        .transpose(2, 0, 1)
    )


def key_terms(group_keys, group_values, group_gates, group_betas):
    cumulative = jnp.cumsum(group_gates, axis=-1)
    row_ids = lax.broadcasted_iota(jnp.int32, (GROUP, GROUP), 0)
    col_ids = lax.broadcasted_iota(jnp.int32, (GROUP, GROUP), 1)
    within = row_ids >= col_ids
    spread = jnp.where(
        within,
        jnp.exp(jnp.where(within, cumulative[..., :, None] - cumulative[..., None, :], 0.0)),
        0.0,
    )
    intersection = jnp.einsum(
        "...id,...jd->...ij", group_keys, group_keys, preferred_element_type=jnp.float32
    )
    keys_wide = group_keys.astype(jnp.float32)
    lower_part = (
        jnp.where(row_ids > col_ids, intersection * spread, 0.0) * group_betas[..., :, None]
    )
    system = lower_part + jnp.eye(GROUP, dtype=jnp.float32)
    scaled = (
        jnp.concatenate([group_values, keys_wide * jnp.exp(cumulative)[..., None]], axis=-1)
        * group_betas[..., None]
    )
    solved = jax.scipy.linalg.solve_triangular(system, scaled, lower=True, unit_diagonal=True)
    head_width = group_keys.shape[-1]
    pseudo = solved[..., :head_width]
    erasers = solved[..., head_width:]
    final_log = cumulative[..., -1:]
    carried = keys_wide * jnp.exp(final_log - cumulative)[..., None]
    return (cumulative, spread, pseudo, erasers, carried, jnp.exp(final_log[..., 0]))


def local(queries, keys, values, log_decay, beta, norm_gain):
    head_queries, head_keys, head_values, head_gates, head_betas = (
        lax.all_to_all(queries, "head", split_axis=1, concat_axis=0, tiled=True),
        lax.all_to_all(keys, "head", split_axis=1, concat_axis=0, tiled=True),
        lax.all_to_all(values, "head", split_axis=1, concat_axis=0, tiled=True),
        lax.all_to_all(log_decay, "head", split_axis=1, concat_axis=0, tiled=True),
        lax.all_to_all(beta, "head", split_axis=1, concat_axis=0, tiled=True),
    )
    token_count, head_count, head_width = head_keys.shape
    group_keys = grouped(unit_rows(head_keys).astype(jnp.bfloat16))
    group_values = grouped(head_values.astype(jnp.float32))
    cumulative, spread, pseudo, erasers, carried, decays = key_terms(
        group_keys, group_values, grouped_gate(head_gates), grouped_gate(head_betas)
    )
    identity = jnp.eye(head_width, dtype=jnp.float32)
    linear_maps = decays[..., None, None] * identity - jnp.einsum(
        "...cd,...ce->...de", carried, erasers, precision=HIGH
    )
    offset_maps = jnp.einsum("...cd,...ce->...de", carried, pseudo, precision=HIGH)
    sections = []
    while linear_maps.shape[1] > 1:
        sections.append((linear_maps, offset_maps))
        linear_maps, offset_maps = compose(
            (linear_maps[:, 0::2], offset_maps[:, 0::2]),
            (linear_maps[:, 1::2], offset_maps[:, 1::2]),
        )
    slab_linear = linear_maps[:, 0]
    slab_offset = offset_maps[:, 0]
    group_queries = grouped((unit_rows(head_queries) * head_width ** (-0.5)).astype(jnp.bfloat16))
    scores = (
        jnp.einsum(
            "...id,...jd->...ij", group_queries, group_keys, preferred_element_type=jnp.float32
        )
        * spread
    )
    gated_queries = group_queries.astype(jnp.float32) * jnp.exp(cumulative)[..., None]
    zero_state = jnp.zeros((head_count, head_width, head_width), jnp.float32)
    prefix = prefix_2(
        (slab_linear, slab_offset),
        "seq",
        compose,
        (jnp.broadcast_to(identity, zero_state.shape), zero_state),
    )
    entry = prefix[1]
    states = entry[:, None]
    for section_linear, section_offset in reversed(sections):
        odd_states = multiply(section_linear[:, 0::2], states) + section_offset[:, 0::2]
        states = jnp.stack([states, odd_states], axis=2).reshape(section_linear.shape)
    residue = pseudo - multiply(erasers, states)
    core = multiply(gated_queries, states) + jnp.einsum(
        "...ij,...je->...ie", scores, residue, precision=HIGH
    )
    scale_rows = lax.rsqrt(jnp.mean(core * core, axis=-1, keepdims=True) + 1e-06)
    normed = (core * scale_rows * norm_gain).astype(jnp.bfloat16)
    normed = normed.transpose(1, 2, 0, 3).reshape(token_count, head_count, head_width)
    return lax.all_to_all(normed, "head", split_axis=0, concat_axis=1, tiled=True)


def solution(mesh):
    placed = (
        P(("seq", "head"), None, None),
        P(("seq", "head"), None, None),
        P(("seq", "head"), None, None),
        P(("seq", "head"), None),
        P(("seq", "head"), None),
        P(),
    )
    return jax.shard_map(
        local, mesh=mesh, in_specs=placed, out_specs=P(("seq", "head"), None, None), check_vma=False
    )
```

profile of v0, /device:TPU:1, one launch (start us, length us, event | category | flops | bytes accessed | tf_op | source)
XLA Modules:
  0.0 354.9 jit_solution(472746820826363098)
XLA Ops:
  6.5 1.3 copy.48
  7.8 7.6 %all-to-all-start.1 = ((bf16[64,16,1]{0,2,1:T(2,128)(2,1)}), bf16[64,16,1]{0,2,1:T(2,128)(2,1)S(1)}, u32[]{:S(2)}, u32[]{:S(2)}) async-start(bf16[64,16,1]{0,2,1:T(2,128)(2,1)} %copy.48), calls=%async_computation.1 | async-start | bytes 16384 | tf_op jit(solution)/shard_map/all_to_all | solution.py:89
  15.5 1.3 copy.50
  16.8 5.0 %all-to-all-done.1 = bf16[64,16,1]{0,2,1:T(2,128)(2,1)S(1)} async-done(((bf16[64,16,1]{0,2,1:T(2,128)(2,1)}), bf16[64,16,1]{0,2,1:T(2,128)(2,1)S(1)}, u32[]{:S(2)}, u32[]{:S(2)}) %all-to-all-start.1) | async-done | bytes 2080 | tf_op jit(solution)/shard_map/all_to_all | solution.py:89
  21.8 3.4 all-to-all-start.3
  25.2 1.7 copy.49
  26.9 1.7 copy.51
  28.9 2.7 all-to-all-done.3
  31.6 3.9 %all-to-all-start.2 = ((bf16[64,16,128]{2,0,1:T(8,128)(2,1)}), bf16[64,16,128]{2,0,1:T(8,128)(2,1)S(1)}, u32[]{:S(2)}, u32[]{:S(2)}) async-start(bf16[64,16,128]{2,0,1:T(8,128)(2,1)} %copy.49), calls=%async_computation.2 | async-start | bytes 524288 | tf_op jit(solution)/shard_map/all_to_all | solution.py:87
  35.8 7.0 %all-to-all-done.2 = bf16[64,16,128]{2,0,1:T(8,128)(2,1)S(1)} async-done(((bf16[64,16,128]{2,0,1:T(8,128)(2,1)}), bf16[64,16,128]{2,0,1:T(8,128)(2,1)S(1)}, u32[]{:S(2)}, u32[]{:S(2)}) %all-to-all-start.2) | async-done | bytes 262176 | tf_op jit(solution)/shard_map/all_to_all | solution.py:87
  42.8 3.5 all-to-all-start.4
  47.3 78.6 %custom-call.4 = f32[16,1,64,64]{2,3,1,0:T(8,128)S(1)} custom-call(f32[16,1,64,64]{3,2,1,0:T(8,128)S(1)} %fusion.18), custom_call_target="InvertDiagBlocksLowerTriangular" | custom-call | tf_op jit(solution)/shard_map/jit(_solve_triangular)/vmap()/triangular_solve | solution.py:75
  126.4 1.3 convolution_bitcast_fusion.1
  127.7 2.2 fusion.10
  130.5 2.1 convolution_bitcast_fusion
  139.7 6.6 %all-to-all-start = ((bf16[64,16,128]{2,0,1:T(8,128)(2,1)}), bf16[64,16,128]{2,0,1:T(8,128)(2,1)S(1)}, u32[]{:S(2)}, u32[]{:S(2)}) async-start(bf16[64,16,128]{2,0,1:T(8,128)(2,1)} %copy.47), calls=%async_computation | async-start | bytes 524288 | tf_op jit(solution)/shard_map/all_to_all | solution.py:86
  146.3 7.3 %all-to-all-done = bf16[64,16,128]{2,0,1:T(8,128)(2,1)S(1)} async-done(((bf16[64,16,128]{2,0,1:T(8,128)(2,1)}), bf16[64,16,128]{2,0,1:T(8,128)(2,1)S(1)}, u32[]{:S(2)}, u32[]{:S(2)}) %all-to-all-start) | async-done | bytes 262176 | tf_op jit(solution)/shard_map/all_to_all | solution.py:86
  153.9 2.1 convolution_multiply_fusion
  156.0 62.1 %all-gather.4.cloned.1.call-done = f32[32,1,128,128]{3,2,1,0:T(8,128)} async-done(((f32[1,1,128,128]{3,2,1,0:T(8,128)}), f32[32,1,128,128]{3,2,1,0:T(8,128)}) %all-gather.4.cloned.1.call-update) | async-done | bytes 2097168 | tf_op jit(solution)/shard_map/all_gather | solution.py:14
  218.1 70.6 %all-gather.6.cloned.1.call-done = f32[4096,128]{1,0:T(8,128)} async-done(((f32[128,128]{1,0:T(8,128)}), f32[4096,128]{1,0:T(8,128)}) %all-gather.6.cloned.1.call-update) | async-done | bytes 2097168 | tf_op jit(solution)/shard_map/all_gather | solution.py:14
  288.7 35.0 %while.14 = (s32[]{:T(128)}, f32[1,128,128]{2,1,0:T(8,128)S(1)}, s32[]{:T(128)}, f32[32,1,128,128]{3,2,1,0:T(8,128)}, f32[32,1,128,128]{3,2,1,0:T(8,128)}, /*index=5*/s32[]{:T(128)}, s32[]{:T(128)}) while((s32[]{:T(128)}, f32[1,128,128]{2,1,0:T(8,128)S(1)}, s32[]{:T(128)}, f32[32,1,128,128]{3,2,1,0:T(8,128)}, ...), condition=%wide.region_4.5_spmd.clone, body=%wide.region_3.4_spmd.clone.sunk | while | flops 25231364 | bytes 461407 | solution.py:23
  293.2 1.1 fusion.110
  301.1 1.1 fusion.110
  306.8 1.1 fusion.110
  307.9 1.1 fusion.110
  313.6 1.1 fusion.110
  321.5 1.1 fusion.110
  323.7 1.1 fusion.30
  324.9 1.2 fusion.27
  328.1 1.1 fusion.12
  329.9 1.3 multiply_reduce_fusion
  332.9 14.0 %all_to_all.71 = bf16[16,2,4096]{2,1,0:T(2,128)(2,1)S(1)} all-to-all(bf16[16,2,4096]{2,1,0:T(2,128)(2,1)S(1)} %reshape.434), channel_id=1, replica_groups=mesh['seq'=32,'head'=16] {'head'}, dimensions={0} | all-to-all | bytes 524288 | tf_op jit(solution)/shard_map/all_to_all | solution.py:139
  (133 shorter events, 42.5 us)
Async XLA Ops:
  7.8 13.9 %all-to-all-start.1 = ((bf16[64,16,1]{0,2,1:T(2,128)(2,1)}), bf16[64,16,1]{0,2,1:T(2,128)(2,1)S(1)}, u32[]{:S(2)}, u32[]{:S(2)}) async-start(bf16[64,16,1]{0,2,1:T(2,128)(2,1)} %copy.48), calls=%async_computation.1 | async-start | bytes 16384 | tf_op jit(solution)/shard_map/all_to_all | solution.py:89
  21.8 9.8 %all-to-all-start.3 = ((bf16[64,16,1]{0,2,1:T(2,128)(2,1)}), bf16[64,16,1]{0,2,1:T(2,128)(2,1)S(1)}, u32[]{:S(2)}, u32[]{:S(2)}) async-start(bf16[64,16,1]{0,2,1:T(2,128)(2,1)} %copy.50), calls=%async_computation.3 | async-start | bytes 16384 | tf_op jit(solution)/shard_map/all_to_all | solution.py:90
  25.2 22.1 %copy-start.11 = (pred[64,64]{1,0:T(8,128)(4,1)}, pred[64,64]{1,0:T(8,128)(4,1)S(1)}, u32[]{:S(2)}) copy-start(pred[64,64]{1,0:T(8,128)(4,1)S(1)} %iota_compare_fusion.3) | copy-start | bytes 12292
  28.9 97.4 %copy-start.10 = (f32[1,16,64]{2,1,0:T(8,128)}, f32[1,16,64]{2,1,0:T(8,128)S(1)}, u32[]{:S(2)}) copy-start(f32[1,16,64]{2,1,0:T(8,128)S(1)} %reduce_window_sum.13) | copy-start | bytes 12292
  31.6 11.2 %all-to-all-start.2 = ((bf16[64,16,128]{2,0,1:T(8,128)(2,1)}), bf16[64,16,128]{2,0,1:T(8,128)(2,1)S(1)}, u32[]{:S(2)}, u32[]{:S(2)}) async-start(bf16[64,16,128]{2,0,1:T(8,128)(2,1)} %copy.49), calls=%async_computation.2 | async-start | bytes 524288 | tf_op jit(solution)/shard_map/all_to_all | solution.py:87
  42.8 83.5 %all-to-all-start.4 = ((bf16[64,16,128]{2,0,1:T(8,128)(2,1)}), bf16[64,16,128]{2,0,1:T(8,128)(2,1)S(1)}, u32[]{:S(2)}, u32[]{:S(2)}) async-start(bf16[64,16,128]{2,0,1:T(8,128)(2,1)} %copy.51), calls=%async_computation.4 | async-start | bytes 524288 | tf_op jit(solution)/shard_map/all_to_all | solution.py:88
  46.4 171.8 %all-gather.4.cloned.1.call-start = ((), (), s32[]{:S(2)}) async-start(), calls=%async_computation.6 | async-start | bytes 2162688 | tf_op jit(solution)/shard_map/all_gather | solution.py:14
  132.7 1.0 copy-start
  133.6 5.3 %copy-start.9 = (bf16[64,16,128]{2,1,0:T(8,128)(2,1)S(1)}, bf16[64,16,128]{2,1,0:T(8,128)(2,1)}, u32[]{:S(2)}) copy-start(bf16[64,16,128]{2,1,0:T(8,128)(2,1)} %param.8) | copy-start | bytes 786436
  134.3 0.8 copy-start.2
  135.6 0.7 copy-start.6
  136.3 3.5 copy-start.4
  136.5 0.7 copy-start.8
  138.0 150.7 %all-gather.6.cloned.1.call-start = ((), (), s32[]{:S(2)}) async-start(), calls=%async_computation.7 | async-start | bytes 2162688 | tf_op jit(solution)/shard_map/all_gather | solution.py:14
  139.7 13.9 %all-to-all-start = ((bf16[64,16,128]{2,0,1:T(8,128)(2,1)}), bf16[64,16,128]{2,0,1:T(8,128)(2,1)S(1)}, u32[]{:S(2)}, u32[]{:S(2)}) async-start(bf16[64,16,128]{2,0,1:T(8,128)(2,1)} %copy.47), calls=%async_computation | async-start | bytes 524288 | tf_op jit(solution)/shard_map/all_to_all | solution.py:86
  156.0 167.7 %copy-start.5 = (f32[1,2,128,128]{3,2,1,0:T(8,128)S(1)}, f32[1,2,128,128]{3,2,1,0:T(8,128)}, u32[]{:S(2)}) copy-start(f32[1,2,128,128]{3,2,1,0:T(8,128)} %copy-done.4) | copy-start | bytes 393220
  323.7 2.4 copy-start.3
  326.0 1.2 copy-start.1
  328.0 1.2 copy-start.7
  329.2 2.0 copy-start.12
Sparse Core Ops, SparseCore 0:
  138.2 79.9 all-gather.3
  220.2 68.4 all-gather.5
where the time goes:
time: 357 us; the launch traced here: 355 us
  waiting for transfers between devices  155 us (43%)
  other arithmetic  81.1 us (23%)
  matrix products  52.7 us (15%)
  starting transfers between devices  25.1 us (7%)
  blocking collectives  14 us (4%)
  between operations  13.9 us (4%)
  local copies, waits for them, and re-layouts  12.2 us (3%)
    all_gather x2, waiting for transfers between devices, prefix_2(): pieces = jax.tree.map(lambda part: lax.all_gather(part, axis), value)  133 us
    another operation x2, other arithmetic, key_terms(): jax.scipy.linalg.solve_triangular(system, scaled, lower=True, unit_diagon...  78.6 us
    dot_general x45, matrix products, multiply(): return jnp.einsum('...ij,...jk->...ik', left, right, precision=HIGH)  43.7 us
    all_to_all x1, blocking collectives, local(): lax.all_to_all(normed, 'head', split_axis=0, concat_axis=1, tiled=True)  14 us
    unnamed x32, local copies, waits for them, and re-layouts  7.73 us
    all_to_all x1, starting transfers between devices, local(): lax.all_to_all(log_decay, 'head', split_axis=1, concat_axis=0, tiled=True)  7.57 us
    all_to_all x1, waiting for transfers between devices, local(): lax.all_to_all(queries, 'head', split_axis=1, concat_axis=0, tiled=True)  7.3 us
  transfers between devices with their start and end apart: 7, of which 6 were waited for; matrix products, arithmetic and copies ran while one was open for 25% of the time, Pallas kernels for 0%

commit v1 on v0

v1 whole, which is shorter than its diff:
```python
import jax
import jax.numpy as jnp
from jax import lax
from jax.experimental import pallas as pl
from jax.experimental.pallas import tpu as pltpu
from jax.sharding import PartitionSpec as P

D = 128
TOK = 64
HEADS = 16
SLAB = TOK * HEADS
CHUNK = 128
CHUNKS = SLAB // CHUNK
KEY, VALUE, QUERY, GATE, ROWS = 0, 64, 128, 192, 200
F32, BF16 = jnp.float32, jnp.bfloat16
VMEM = pl.BlockSpec(memory_space=pltpu.VMEM)
SMEM = pl.BlockSpec(memory_space=pltpu.SMEM)


def mm(left, right):
    return jnp.dot(left, right, preferred_element_type=F32)


def mm_nt(left, right):
    return lax.dot_general(left, right, (((1,), (1,)), ((), ())), preferred_element_type=F32)


def mm_tn(left, right):
    return lax.dot_general(left, right, (((0,), (0,)), ((), ())), preferred_element_type=F32)


def split(value):
    high = value.astype(BF16)
    return high, (value - high.astype(F32)).astype(BF16)


def wide(value):
    return jnp.concatenate(split(value), axis=1)


def tall(value):
    return jnp.concatenate(split(value), axis=0)


def twice(value, axis):
    return jnp.concatenate([value, value], axis=axis)


def square(value):
    high, low = split(value)
    top = jnp.concatenate([high, low], axis=1)
    bottom = jnp.concatenate([high, jnp.zeros_like(high)], axis=1)
    return jnp.concatenate([top, bottom], axis=0)


def halves(value):
    return value[:, :D] + value[:, D:]


def mm3(left, right):
    return halves(mm(wide(left), square(right)))


def mm3_wide(left, right):
    high, low = split(right)
    left_high, left_low = split(left)
    both = jnp.concatenate([left_high, left_low], axis=1)
    return mm(both, twice(high, 0)) + mm(left_high, low)


def iotas(rows, columns):
    shape = (rows, columns)
    return lax.broadcasted_iota(jnp.int32, shape, 0), lax.broadcasted_iota(jnp.int32, shape, 1)


def ones_where(condition):
    return jnp.where(condition, 1.0, 0.0).astype(BF16)


def gates(received):
    rows = received[:, GATE:ROWS, :].astype(F32)[:, 0, :].astype(BF16)
    chunk_ids, source_ids = iotas(CHUNKS, HEADS)
    even = mm(ones_where(source_ids == 2 * chunk_ids), rows).astype(BF16)
    odd = mm(ones_where(source_ids == 2 * chunk_ids + 1), rows).astype(BF16)
    to, at = iotas(CHUNK, D)
    sum_even = ones_where((at < TOK) & (at <= to))
    sum_odd = ones_where((at < TOK) & (at + TOK <= to))
    beta_even = ones_where((to < TOK) & (at == to + TOK))
    beta_odd = ones_where((to >= TOK) & (at == to))
    log_rows = mm_nt(even, sum_even) + mm_nt(odd, sum_odd)
    log_columns = mm_nt(sum_even, even) + mm_nt(sum_odd, odd)
    beta_rows = mm_nt(even, beta_even) + mm_nt(odd, beta_odd)
    beta_columns = mm_nt(beta_even, even) + mm_nt(beta_odd, odd)
    return log_rows, log_columns, beta_rows, beta_columns


def part(received, chunk, offset):
    return received[2 * chunk : 2 * chunk + 2, offset : offset + TOK, :].reshape(CHUNK, D)


def spread_of(log_rows, log_columns, chunk, row_ids, column_ids):
    difference = log_columns[:, chunk : chunk + 1] - log_rows[chunk : chunk + 1, :]
    return jnp.exp(jnp.where(row_ids >= column_ids, difference, -1e30))


def pack_kernel(queries, keys, values, log_decay, beta, sent, key_rows, value_rows, query_rows):
    wide_keys = keys[...].reshape(SLAB, D).astype(F32)
    total = jnp.sum(wide_keys * wide_keys, axis=1, keepdims=True)
    key_rows[...] = wide_keys * lax.rsqrt(total + 1e-06)
    value_rows[...] = values[...].reshape(SLAB, D).astype(F32)
    query_rows[...] = queries[...].reshape(SLAB, D).astype(F32)
    to, at = iotas(TOK, D)
    rows = mm_tn(log_decay[...], ones_where(at == to)) + mm_tn(beta[...], ones_where(at == to + TOK))
    for head in range(HEADS):
        pick = pl.ds(head, TOK, stride=HEADS)
        sent[head, KEY : KEY + TOK, :] = key_rows[pick, :].astype(BF16)
        sent[head, VALUE : VALUE + TOK, :] = value_rows[pick, :].astype(BF16)
        sent[head, QUERY : QUERY + TOK, :] = query_rows[pick, :].astype(BF16)
        sent[head, GATE:ROWS, :] = jnp.broadcast_to(rows[head : head + 1, :], (8, D)).astype(BF16)


def map_kernel(received, sent, prefixes, solved):
    log_rows, log_columns, beta_rows, beta_columns = gates(received)
    row_ids, column_ids = iotas(CHUNK, CHUNK)
    apart = row_ids ^ column_ids
    eye = jnp.where(apart == 0, 1.0, 0.0)
    lowers, inverses = [], []
    for c in range(CHUNKS):
        keys = part(received, c, KEY)
        spread = spread_of(log_rows, log_columns, c, row_ids, column_ids)
        lower = jnp.where(row_ids > column_ids, mm_nt(keys, keys) * spread, 0.0)
        lower = lower * beta_columns[:, c : c + 1]
        lowers.append(lower)
        inverses.append(eye - jnp.where(apart == 1, lower, 0.0))
    for level in range(1, 7):
        mask = (apart >> level) == 1
        for c in range(CHUNKS):
            inverse = inverses[c]
            inner = mm3(inverse, jnp.where(mask, lowers[c], 0.0))
            inverses[c] = inverse - mm3(inner, inverse)
    log_scale = jnp.exp(log_rows)
    prefix = None
    for c in range(CHUNKS):
        keys, values = part(received, c, KEY), part(received, c, VALUE)
        inverse = inverses[c] * beta_rows[c : c + 1, :]
        erasers = mm(wide(inverse * log_scale[c : c + 1, :]), twice(keys, 0))
        pseudo = mm(wide(inverse), twice(values, 0))
        both = jnp.concatenate([erasers, pseudo], axis=1)
        solved[c] = both
        last = log_rows[c : c + 1, CHUNK - 1 : CHUNK]
        carried = both * jnp.exp(last - log_columns[:, c : c + 1])
        maps = mm_tn(twice(keys, 0), tall(carried))
        linear = eye * jnp.exp(last) - maps[:, :D]
        offset = maps[:, D:]
        if prefix is None:
            prefixes[c] = jnp.concatenate([eye, jnp.zeros_like(eye)], axis=1)
            prefix = jnp.concatenate([linear, offset], axis=1)
        else:
            prefixes[c] = prefix
            moved = mm3_wide(linear, prefix)
            prefix = jnp.concatenate([moved[:, :D], moved[:, D:] + offset], axis=1)
    for copy in range(4):
        sent[copy] = prefix.astype(BF16)


def query_kernel(received, prefixes, solved, query_maps, base):
    log_rows, log_columns, _, _ = gates(received)
    row_ids, column_ids = iotas(CHUNK, CHUNK)
    for c in range(CHUNKS):
        keys = part(received, c, KEY)
        raw = part(received, c, QUERY).astype(F32)
        total = jnp.sum(raw * raw, axis=1, keepdims=True)
        queries = (raw * lax.rsqrt(total + 1e-06) * D**-0.5).astype(BF16)
        spread = spread_of(log_rows, log_columns, c, row_ids, column_ids)
        scores = mm_nt(queries, keys) * spread
        prefix, both = prefixes[c], solved[c]
        erased = mm3_wide(both[:, :D], prefix)
        residue = jnp.concatenate([-erased[:, :D], both[:, D:] - erased[:, D:]], axis=1)
        direct = mm(twice(queries, 1), tall(prefix)) * jnp.exp(log_columns[:, c : c + 1])
        result = direct + mm3_wide(scores, residue)
        query_maps[c * CHUNK : (c + 1) * CHUNK, :] = wide(result[:, :D])
        base[c * CHUNK : (c + 1) * CHUNK, :] = result[:, D:]


def block_kernel(place, received, before, total):
    eye = jnp.where(jnp.equal(*iotas(D, D)), 1.0, 0.0)
    prefix = jnp.concatenate([eye, jnp.zeros_like(eye)], axis=1)
    chosen = prefix
    for p in range(4):
        if p:
            chosen = jnp.where(place[0] == p, prefix, chosen)
        linear = received[p, :, :D]
        if p == 0:
            prefix = received[p].astype(F32)
        else:
            moved = mm(twice(linear, 1), tall(prefix))
            offset = received[p, :, D:].astype(F32)
            prefix = jnp.concatenate([moved[:, :D], moved[:, D:] + offset], axis=1)
    before[...] = chosen
    total[...] = prefix.astype(BF16)


def join_kernel(total, earlier, joined):
    moved = mm(total[:, :D], earlier[...])
    joined[:, :D] = moved[:, :D].astype(BF16)
    joined[:, D:] = (moved[:, D:] + total[:, D:].astype(F32)).astype(BF16)


def shift_kernel(before, earlier, query_maps, base, shifted_maps, shifted_base):
    first = before[...]
    moved = mm(wide(first[:, :D]), twice(earlier[...], 0))
    prefix = jnp.concatenate([moved[:, :D], moved[:, D:] + first[:, D:]], axis=1)
    high, low = split(prefix)
    for c in range(4):
        rows = slice(c * 256, (c + 1) * 256)
        maps = query_maps[rows, :]
        result = mm(maps, twice(high, 0)) + mm(maps[:, :D], low)
        shifted_maps[rows, :] = wide(result[:, :D])
        shifted_base[rows, :] = base[rows, :] + result[:, D:]


def output_kernel(near, far, farthest, query_maps, base, gain, sent):
    state = farthest[...].astype(F32)
    state = mm(twice(far[:, :D], 1), tall(state)) + far[:, D:].astype(F32)
    state = mm(twice(near[:, :D], 1), tall(state)) + near[:, D:].astype(F32)
    weights = square(state)
    for c in range(4):
        rows = slice(c * 256, (c + 1) * 256)
        core = halves(mm(query_maps[rows, :], weights)) + base[rows, :]
        scale = lax.rsqrt(jnp.mean(core * core, axis=1, keepdims=True) + 1e-06)
        sent[rows, :] = (core * scale * gain[...]).astype(BF16)


def unpack_kernel(received, out, rows):
    rows[...] = received[...].reshape(SLAB, D).astype(F32)
    for token in range(TOK):
        out[token] = rows[pl.ds(token, HEADS, stride=TOK), :].astype(BF16)


def call(kernel, outs, *operands, scratch=(), flops=0, scalars=0):
    outs = [jax.ShapeDtypeStruct(shape, dtype) for shape, dtype in outs]
    size = sum(a.size * a.dtype.itemsize for a in operands)
    return pl.pallas_call(
        kernel,
        out_shape=outs if len(outs) > 1 else outs[0],
        in_specs=[SMEM] * scalars + [VMEM] * (len(operands) - scalars),
        out_specs=[VMEM] * len(outs) if len(outs) > 1 else VMEM,
        scratch_shapes=scratch,
        compiler_params=pltpu.CompilerParams(vmem_limit_bytes=24 << 20),
        cost_estimate=pl.CostEstimate(flops=flops, bytes_accessed=size, transcendentals=0),
        name=kernel.__name__,
    )(*operands)


def local(queries, keys, values, log_decay, beta, norm_gain):
    rows = pltpu.VMEM((SLAB, D), F32)
    packed = call(
        pack_kernel,
        [((HEADS, ROWS, D), BF16)],
        queries,
        keys,
        values,
        log_decay,
        beta,
        scratch=[rows, rows, rows],
    )
    received = lax.all_to_all(packed, "head", 0, 0, tiled=True)
    maps, prefixes, solved = call(
        map_kernel,
        [((4, D, 2 * D), BF16), ((CHUNKS, D, 2 * D), F32), ((CHUNKS, CHUNK, 2 * D), F32)],
        received,
        flops=1 << 33,
    )
    count = lax.axis_size("seq")
    groups = [[first + p for p in range(4)] for first in range(0, count, 4)]
    block = lax.all_to_all(maps, "seq", 0, 0, axis_index_groups=groups, tiled=True)
    query_maps, base = call(
        query_kernel,
        [((SLAB, 2 * D), BF16), ((SLAB, D), F32)],
        received,
        prefixes,
        solved,
        flops=1 << 33,
    )
    place = (lax.axis_index("seq") % 4).astype(jnp.int32).reshape(1)
    before, total = call(
        block_kernel, [((D, 2 * D), F32), ((D, 2 * D), BF16)], place, block, scalars=1
    )

    def moved(value, by):
        return lax.ppermute(value, "seq", [(s, s + by) for s in range(count - by)])

    earlier = moved(total, 4)
    joined = call(join_kernel, [((D, 2 * D), BF16)], total, earlier)
    near, far, farthest = moved(joined, 8), moved(joined, 16), moved(joined[:, D:], 24)
    query_maps, base = call(
        shift_kernel,
        [((SLAB, 2 * D), BF16), ((SLAB, D), F32)],
        before,
        earlier,
        query_maps,
        base,
        flops=1 << 31,
    )
    normed = call(
        output_kernel,
        [((SLAB, D), BF16)],
        near,
        far,
        farthest,
        query_maps,
        base,
        norm_gain.reshape(1, D),
    )
    returned = lax.all_to_all(normed.reshape(HEADS, TOK, D), "head", 0, 0, tiled=True)
    return call(unpack_kernel, [((TOK, HEADS, D), BF16)], returned, scratch=[rows])


def solution(mesh):
    rows = P(("seq", "head"), None, None)
    columns = P(("seq", "head"), None)
    return jax.shard_map(
        local,
        mesh=mesh,
        in_specs=(rows, rows, rows, columns, columns, P()),
        out_specs=rows,
        check_vma=False,
    )
```

time: 357 us -> 89.3 us (0.25)
  waiting for transfers between devices: 155 us -> 10 us
  other arithmetic: 81.1 us -> 0 us
  matrix products: 52.7 us -> 0 us
  blocking collectives: 14 us -> 29.9 us
  between operations: 13.9 us -> 0.1 us
  Pallas kernels: 0 us -> 10.5 us
  starting transfers between devices: 25.1 us -> 33.9 us
  local copies, waits for them, and re-layouts: 12.2 us -> 4.41 us
    all_gather x2 -> x0, waiting for transfers between devices: 133 us -> none  [prefix_2(): pieces = jax.tree.map(lambda part: lax.all_gather(part, axis), value)]
    another operation x8 -> x0, other arithmetic: 79.8 us -> none  [the longest x2 78.6 us: key_terms(): jax.scipy.linalg.solve_triangular(system, scaled, lower=True, unit_diagon...]
    dot_general x50 -> x0, matrix products: 51.5 us -> none  [the longest x45 43.7 us: multiply(): return jnp.einsum('...ij,...jk->...ik', left, right, precision=HIGH)]
    ppermute x0 -> x4, starting transfers between devices: none -> 27 us  [moved(): return lax.ppermute(value, 'seq', [(s, s + by) for s in range(count - by)])]
    all_to_all x5 -> x1, starting transfers between devices: 25 us -> 6.91 us  [local(): lax.all_to_all(maps, 'seq', 0, 0, axis_index_groups=groups, tiled=True)]
    all_to_all x5 -> x1, waiting for transfers between devices: 22 us -> 5.04 us  [local(): lax.all_to_all(maps, 'seq', 0, 0, axis_index_groups=groups, tiled=True)]
    all_to_all x1 -> x2, blocking collectives: 14 us -> 29.9 us  [the longest x1 19.2 us: local(): received = lax.all_to_all(packed, 'head', 0, 0, tiled=True)]
    pallas_call x0 -> x8, Pallas kernels: none -> 10.5 us  [call(): pl.pallas_call(kernel, out_shape=outs if len(outs) > 1 else outs[0], in_s...]
  transfers between devices with their start and end apart: 7 -> 5, of which waited for: 6 -> 2; matrix products, arithmetic and copies ran while one was open for 25% -> 0% of each run, Pallas kernels for 0% -> 3%
where the time goes in v1:
time: 89.3 us; the launch traced here: 88.8 us
  starting transfers between devices  33.9 us (38%)
  blocking collectives  29.9 us (33%)
  Pallas kernels  10.5 us (12%)
  waiting for transfers between devices  10 us (11%)
  local copies, waits for them, and re-layouts  4.41 us (5%)
    ppermute x4, starting transfers between devices, moved(): return lax.ppermute(value, 'seq', [(s, s + by) for s in range(count - by)])  27 us
    all_to_all x1, blocking collectives, local(): received = lax.all_to_all(packed, 'head', 0, 0, tiled=True)  19.2 us
    all_to_all x1, blocking collectives, local(): lax.all_to_all(normed.reshape(HEADS, TOK, D), 'head', 0, 0, tiled=True)  10.7 us
    pallas_call x8, Pallas kernels, call(): pl.pallas_call(kernel, out_shape=outs if len(outs) > 1 else outs[0], in_s...  10.5 us
    all_to_all x1, starting transfers between devices, local(): lax.all_to_all(maps, 'seq', 0, 0, axis_index_groups=groups, tiled=True)  6.91 us
    all_to_all x1, waiting for transfers between devices, local(): lax.all_to_all(maps, 'seq', 0, 0, axis_index_groups=groups, tiled=True)  5.04 us
    ppermute x4, waiting for transfers between devices, moved(): return lax.ppermute(value, 'seq', [(s, s + by) for s in range(count - by)])  4.97 us
    unnamed x12, local copies, waits for them, and re-layouts  4.4 us
  transfers between devices with their start and end apart: 5, of which 2 were waited for; matrix products, arithmetic and copies ran while one was open for 0% of the time, Pallas kernels for 3%

profile of v1, /device:TPU:1, one launch (start us, length us, event | category | flops | bytes accessed | tf_op | source)
XLA Modules:
  0.0 88.8 jit_solution(12342621263357989432)
XLA Ops:
  0.0 0.0 copy-start.4
  0.0 0.8 copy.7.log_decay
  0.8 0.0 copy-done.4
  0.8 0.1 copy.8.beta
  0.9 0.0 copy-start
  0.9 0.9 %copy-done = bf16[64,16,128]{2,1,0:T(8,128)(2,1)S(1)} copy-done((bf16[64,16,128]{2,1,0:T(8,128)(2,1)S(1)}, bf16[64,16,128]{2,1,0:T(8,128)(2,1)}, u32[]{:S(2)}) %copy-start) | copy-done | bytes 262168
  1.9 0.0 copy-start.1
  1.9 0.9 %copy-done.1 = bf16[64,16,128]{2,1,0:T(8,128)(2,1)S(1)} copy-done((bf16[64,16,128]{2,1,0:T(8,128)(2,1)S(1)}, bf16[64,16,128]{2,1,0:T(8,128)(2,1)}, u32[]{:S(2)}) %copy-start.1) | copy-done | bytes 262168
  2.8 0.0 copy-start.2
  2.8 0.9 %copy-done.2 = bf16[64,16,128]{2,1,0:T(8,128)(2,1)S(1)} copy-done((bf16[64,16,128]{2,1,0:T(8,128)(2,1)S(1)}, bf16[64,16,128]{2,1,0:T(8,128)(2,1)}, u32[]{:S(2)}) %copy-start.2) | copy-done | bytes 262168
  3.8 0.7 pack_kernel.1
  4.5 19.2 %all_to_all.15.received = bf16[16,200,128]{2,1,0:T(8,128)(2,1)S(1)} all-to-all(bf16[16,200,128]{2,1,0:T(8,128)(2,1)S(1)} %pack_kernel.1), channel_id=1, replica_groups=mesh['seq'=32,'head'=16] {'head'}, dimensions={0} | all-to-all | bytes 1638400 | tf_op jit(solution)/shard_map/all_to_all | solution.py:267
  23.7 5.2 %map_kernel.1 = (bf16[4,128,256]{2,1,0:T(8,128)(2,1)}, f32[8,128,256]{2,1,0:T(8,128)S(1)}, f32[8,128,256]{2,1,0:T(8,128)S(1)}) custom-call(bf16[16,200,128]{2,1,0:T(8,128)(2,1)S(1)} %all_to_all.15.received), custom_call_target="tpu_custom_call" | custom-call | flops 8589934592 | bytes 819200 | tf_op jit(solution)/shard_map/map_kernel/pallas_call | solution.py:243
  28.9 6.9 %all-to-all-start.1 = ((bf16[4,128,256]{2,1,0:T(8,128)(2,1)}), bf16[4,128,256]{2,1,0:T(8,128)(2,1)S(1)}, u32[]{:S(2)}, u32[]{:S(2)}) async-start(bf16[4,128,256]{2,1,0:T(8,128)(2,1)} %get-tuple-element.14), calls=%async_computation.1 | async-start | bytes 524288 | tf_op jit(solution)/shard_map/all_to_all | solution.py:276
  35.8 5.0 %all-to-all-done.1.received = bf16[4,128,256]{2,1,0:T(8,128)(2,1)S(1)} async-done(((bf16[4,128,256]{2,1,0:T(8,128)(2,1)}), bf16[4,128,256]{2,1,0:T(8,128)(2,1)S(1)}, u32[]{:S(2)}, u32[]{:S(2)}) %all-to-all-start.1) | async-done | bytes 262176 | tf_op jit(solution)/shard_map/all_to_all | solution.py:276
  40.8 0.5 block_kernel.1
  41.3 4.9 %collective-permute-start = (bf16[128,256]{1,0:T(8,128)(2,1)S(1)}, bf16[128,256]{1,0:T(8,128)(2,1)S(1)}, u32[]{:S(2)}, u32[]{:S(2)}) collective-permute-start(bf16[128,256]{1,0:T(8,128)(2,1)S(1)} %get-tuple-element.15.total), channel_id=1, source_target_pairs={{0,64},{16,80},{32,96},{48,112},{64,128},{80,144},{96,160},{112,17... | collective-permute-start | bytes 196616 | tf_op jit(solution)/shard_map/ppermute | solution.py:291
  46.2 1.6 %query_kernel.1 = (bf16[1024,256]{1,0:T(8,128)(2,1)S(1)}, f32[1024,128]{1,0:T(8,128)S(1)}) custom-call(bf16[16,200,128]{2,1,0:T(8,128)(2,1)S(1)} %all_to_all.15.received, f32[8,128,256]{2,1,0:T(8,128)S(1)} %get-tuple-element.17.prefixes, f32[8,128,256]{2,1,0:T(8,128)S(1)} %get-tuple-element.18.solved), custom_call_target="tpu_custom_call" | custom-call | flops 8589934592 | bytes 2916352 | tf_op jit(solution)/shard_map/query_kernel/pallas_call | solution.py:243
  47.9 0.0 collective-permute-done.earlier
  47.9 0.1 join_kernel.1
  48.0 9.4 %collective-permute-start.1 = (bf16[128,256]{1,0:T(8,128)(2,1)S(1)}, bf16[128,256]{1,0:T(8,128)(2,1)S(1)}, u32[]{:S(2)}, u32[]{:S(2)}) collective-permute-start(bf16[128,256]{1,0:T(8,128)(2,1)S(1)} %join_kernel.1), channel_id=1, source_target_pairs={{0,128},{16,144},{32,160},{48,176},{64,192},{80,208},{96,224},{112... | collective-permute-start | bytes 196616 | tf_op jit(solution)/shard_map/ppermute | solution.py:291
  57.4 11.4 %collective-permute-start.2 = (bf16[128,256]{1,0:T(8,128)(2,1)S(1)}, bf16[128,256]{1,0:T(8,128)(2,1)S(1)}, u32[]{:S(2)}, u32[]{:S(2)}) collective-permute-start(bf16[128,256]{1,0:T(8,128)(2,1)S(1)} %join_kernel.1), channel_id=1, source_target_pairs={{0,256},{16,272},{32,288},{48,304},{64,320},{80,336},{96,352},{112... | collective-permute-start | bytes 196616 | tf_op jit(solution)/shard_map/ppermute | solution.py:291
  68.8 1.3 %collective-permute-start.3 = (bf16[128,128]{1,0:T(8,128)(2,1)S(1)}, bf16[128,128]{1,0:T(8,128)(2,1)S(1)}, u32[]{:S(2)}, u32[]{:S(2)}) collective-permute-start(bf16[128,128]{1,0:T(8,128)(2,1)S(1)} %slice.4), channel_id=1, source_target_pairs={{0,384},{16,400},{32,416},{48,432},{64,448},{80,464},{96,480},{112... | collective-permute-start | bytes 98312 | tf_op jit(solution)/shard_map/ppermute | solution.py:291
  70.1 0.6 shift_kernel.1
  70.8 5.0 %collective-permute-done.3.farthest = bf16[128,128]{1,0:T(8,128)(2,1)S(1)} collective-permute-done((bf16[128,128]{1,0:T(8,128)(2,1)S(1)}, bf16[128,128]{1,0:T(8,128)(2,1)S(1)}, u32[]{:S(2)}, u32[]{:S(2)}) %collective-permute-start.3) | collective-permute-done | bytes 32800 | tf_op jit(solution)/shard_map/ppermute | solution.py:291
  75.7 0.0 collective-permute-done.1.near
  75.7 0.0 collective-permute-done.2.far
  75.7 0.0 copy-start.3
  75.7 0.7 copy-done.3
  76.4 0.7 output_kernel.1
  77.1 10.7 %all_to_all.16.received = bf16[16,64,128]{2,1,0:T(8,128)(2,1)S(1)} all-to-all(bf16[16,64,128]{2,1,0:T(8,128)(2,1)S(1)} %bitcast.3), channel_id=1, replica_groups=mesh['seq'=32,'head'=16] {'head'}, dimensions={0} | all-to-all | bytes 524288 | tf_op jit(solution)/shard_map/all_to_all | solution.py:315
  87.8 1.0 %unpack_kernel.1 = bf16[64,16,128]{2,1,0:T(8,128)(2,1)} custom-call(bf16[16,64,128]{2,1,0:T(8,128)(2,1)S(1)} %all_to_all.16.received), custom_call_target="tpu_custom_call" | custom-call | bytes 262144 | tf_op jit(solution)/shard_map/unpack_kernel/pallas_call | solution.py:243
  (1 shorter events, 0.0 us)
Async XLA Ops:
  0.0 0.8 copy-start.4
  0.9 1.0 %copy-start = (bf16[64,16,128]{2,1,0:T(8,128)(2,1)S(1)}, bf16[64,16,128]{2,1,0:T(8,128)(2,1)}, u32[]{:S(2)}) copy-start(bf16[64,16,128]{2,1,0:T(8,128)(2,1)} %queries.1) | copy-start | bytes 786436
  1.9 0.9 %copy-start.1 = (bf16[64,16,128]{2,1,0:T(8,128)(2,1)S(1)}, bf16[64,16,128]{2,1,0:T(8,128)(2,1)}, u32[]{:S(2)}) copy-start(bf16[64,16,128]{2,1,0:T(8,128)(2,1)} %keys.1) | copy-start | bytes 786436
  2.8 0.9 %copy-start.2 = (bf16[64,16,128]{2,1,0:T(8,128)(2,1)S(1)}, bf16[64,16,128]{2,1,0:T(8,128)(2,1)}, u32[]{:S(2)}) copy-start(bf16[64,16,128]{2,1,0:T(8,128)(2,1)} %values.1) | copy-start | bytes 786436
  28.9 12.0 %all-to-all-start.1 = ((bf16[4,128,256]{2,1,0:T(8,128)(2,1)}), bf16[4,128,256]{2,1,0:T(8,128)(2,1)S(1)}, u32[]{:S(2)}, u32[]{:S(2)}) async-start(bf16[4,128,256]{2,1,0:T(8,128)(2,1)} %get-tuple-element.14), calls=%async_computation.1 | async-start | bytes 524288 | tf_op jit(solution)/shard_map/all_to_all | solution.py:276
  41.3 6.5 %collective-permute-start = (bf16[128,256]{1,0:T(8,128)(2,1)S(1)}, bf16[128,256]{1,0:T(8,128)(2,1)S(1)}, u32[]{:S(2)}, u32[]{:S(2)}) collective-permute-start(bf16[128,256]{1,0:T(8,128)(2,1)S(1)} %get-tuple-element.15.total), channel_id=1, source_target_pairs={{0,64},{16,80},{32,96},{48,112},{64,128},{80,144},{96,160},{112,17... | collective-permute-start | bytes 196616 | tf_op jit(solution)/shard_map/ppermute | solution.py:291
  48.0 27.7 %collective-permute-start.1 = (bf16[128,256]{1,0:T(8,128)(2,1)S(1)}, bf16[128,256]{1,0:T(8,128)(2,1)S(1)}, u32[]{:S(2)}, u32[]{:S(2)}) collective-permute-start(bf16[128,256]{1,0:T(8,128)(2,1)S(1)} %join_kernel.1), channel_id=1, source_target_pairs={{0,128},{16,144},{32,160},{48,176},{64,192},{80,208},{96,224},{112... | collective-permute-start | bytes 196616 | tf_op jit(solution)/shard_map/ppermute | solution.py:291
  57.4 18.3 %collective-permute-start.2 = (bf16[128,256]{1,0:T(8,128)(2,1)S(1)}, bf16[128,256]{1,0:T(8,128)(2,1)S(1)}, u32[]{:S(2)}, u32[]{:S(2)}) collective-permute-start(bf16[128,256]{1,0:T(8,128)(2,1)S(1)} %join_kernel.1), channel_id=1, source_target_pairs={{0,256},{16,272},{32,288},{48,304},{64,320},{80,336},{96,352},{112... | collective-permute-start | bytes 196616 | tf_op jit(solution)/shard_map/ppermute | solution.py:291
  68.8 6.9 %collective-permute-start.3 = (bf16[128,128]{1,0:T(8,128)(2,1)S(1)}, bf16[128,128]{1,0:T(8,128)(2,1)S(1)}, u32[]{:S(2)}, u32[]{:S(2)}) collective-permute-start(bf16[128,128]{1,0:T(8,128)(2,1)S(1)} %slice.4), channel_id=1, source_target_pairs={{0,384},{16,400},{32,416},{48,432},{64,448},{80,464},{96,480},{112... | collective-permute-start | bytes 98312 | tf_op jit(solution)/shard_map/ppermute | solution.py:291
  75.7 0.7 copy-start.3

commit v2 on v1

--- a/solution.py
+++ b/solution.py
@@ -4,6 +4,7 @@
 from jax.experimental import pallas as pl
 from jax.experimental.pallas import tpu as pltpu
 from jax.sharding import PartitionSpec as P
+
 
 D = 128
 TOK = 64
@@ -103,20 +104,30 @@
     return jnp.exp(jnp.where(row_ids >= column_ids, difference, -1e30))
 
 
-def pack_kernel(queries, keys, values, log_decay, beta, sent, key_rows, value_rows, query_rows):
-    wide_keys = keys[...].reshape(SLAB, D).astype(F32)
-    total = jnp.sum(wide_keys * wide_keys, axis=1, keepdims=True)
-    key_rows[...] = wide_keys * lax.rsqrt(total + 1e-06)
-    value_rows[...] = values[...].reshape(SLAB, D).astype(F32)
-    query_rows[...] = queries[...].reshape(SLAB, D).astype(F32)
+def pack_kernel(*refs):
+    sources, (sent, gains, taken, decays, betas, rows, arrived) = refs[:6], refs[6:]
+    targets = (decays, betas, gains, taken.at[0], taken.at[1], taken.at[2])
+    copies = [
+        pltpu.make_async_copy(source, target, arrived.at[n])
+        for n, (source, target) in enumerate(zip(sources, targets))
+    ]
+    for copy in copies:
+        copy.start()
+    for copy in copies[:3]:
+        copy.wait()
     to, at = iotas(TOK, D)
-    rows = mm_tn(log_decay[...], ones_where(at == to)) + mm_tn(beta[...], ones_where(at == to + TOK))
+    gate_rows = mm(decays[...], ones_where(at == to)) + mm(betas[...], ones_where(at == to + TOK))
     for head in range(HEADS):
-        pick = pl.ds(head, TOK, stride=HEADS)
-        sent[head, KEY : KEY + TOK, :] = key_rows[pick, :].astype(BF16)
-        sent[head, VALUE : VALUE + TOK, :] = value_rows[pick, :].astype(BF16)
-        sent[head, QUERY : QUERY + TOK, :] = query_rows[pick, :].astype(BF16)
-        sent[head, GATE:ROWS, :] = jnp.broadcast_to(rows[head : head + 1, :], (8, D)).astype(BF16)
+        sent[head, GATE:ROWS, :] = jnp.broadcast_to(gate_rows[head : head + 1, :], (8, D)).astype(BF16)
+    for n, offset in enumerate((KEY, VALUE, QUERY)):
+        copies[3 + n].wait()
+        raw = taken[n].reshape(SLAB, D).astype(F32)
+        if n == 0:
+            raw = raw * lax.rsqrt(jnp.sum(raw * raw, axis=1, keepdims=True) + 1e-06)
+        rows[n] = raw
+        for head in range(HEADS):
+            picked = rows[n, pl.ds(head, TOK, stride=HEADS), :]
+            sent[head, offset : offset + TOK, :] = picked.astype(BF16)
 
 
 def map_kernel(received, sent, prefixes, solved):
@@ -237,32 +248,36 @@
         out[token] = rows[pl.ds(token, HEADS, stride=TOK), :].astype(BF16)
 
 
-def call(kernel, outs, *operands, scratch=(), flops=0, scalars=0):
+def call(kernel, outs, *operands, scratch=(), flops=0, scalars=0, raw=0):
     outs = [jax.ShapeDtypeStruct(shape, dtype) for shape, dtype in outs]
     size = sum(a.size * a.dtype.itemsize for a in operands)
     return pl.pallas_call(
         kernel,
         out_shape=outs if len(outs) > 1 else outs[0],
-        in_specs=[SMEM] * scalars + [VMEM] * (len(operands) - scalars),
+        in_specs=[SMEM] * scalars
+        + [pl.BlockSpec(memory_space=pltpu.HBM)] * raw
+        + [VMEM] * (len(operands) - scalars - raw),
         out_specs=[VMEM] * len(outs) if len(outs) > 1 else VMEM,
         scratch_shapes=scratch,
         compiler_params=pltpu.CompilerParams(vmem_limit_bytes=24 << 20),
         cost_estimate=pl.CostEstimate(flops=flops, bytes_accessed=size, transcendentals=0),
-        name=kernel.__name__,
     )(*operands)
 
 
 def local(queries, keys, values, log_decay, beta, norm_gain):
-    rows = pltpu.VMEM((SLAB, D), F32)
-    packed = call(
+    sources = (log_decay.T, beta.T, norm_gain.reshape(1, D), keys, values, queries)
+    packed, gains = call(
         pack_kernel,
-        [((HEADS, ROWS, D), BF16)],
-        queries,
-        keys,
-        values,
-        log_decay,
-        beta,
-        scratch=[rows, rows, rows],
+        [((HEADS, ROWS, D), BF16), ((1, D), F32)],
+        *(pltpu.with_memory_space_constraint(source, pltpu.HBM) for source in sources),
+        scratch=[
+            pltpu.VMEM((3, TOK, HEADS, D), BF16),
+            pltpu.VMEM((HEADS, TOK), BF16),
+            pltpu.VMEM((HEADS, TOK), BF16),
+            pltpu.VMEM((3, SLAB, D), F32),
+            pltpu.SemaphoreType.DMA((6,)),
+        ],
+        raw=6,
     )
     received = lax.all_to_all(packed, "head", 0, 0, tiled=True)
     maps, prefixes, solved = call(
@@ -292,7 +307,9 @@
 
     earlier = moved(total, 4)
     joined = call(join_kernel, [((D, 2 * D), BF16)], total, earlier)
-    near, far, farthest = moved(joined, 8), moved(joined, 16), moved(joined[:, D:], 24)
+    near = moved(joined, 8)
+    far = lax.ppermute(joined, "seq", [(s, (s ^ 2) + 16) for s in range(count - 16)])
+    farthest = moved(joined[:, D:], 24)
     query_maps, base = call(
         shift_kernel,
         [((SLAB, 2 * D), BF16), ((SLAB, D), F32)],
@@ -310,10 +327,10 @@
         farthest,
         query_maps,
         base,
-        norm_gain.reshape(1, D),
+        gains,
     )
     returned = lax.all_to_all(normed.reshape(HEADS, TOK, D), "head", 0, 0, tiled=True)
-    return call(unpack_kernel, [((TOK, HEADS, D), BF16)], returned, scratch=[rows])
+    return call(unpack_kernel, [((TOK, HEADS, D), BF16)], returned, scratch=[pltpu.VMEM((SLAB, D), F32)])
 
 
 def solution(mesh):

time: 89.3 us -> 84.9 us (0.951)
  local copies, waits for them, and re-layouts: 4.41 us -> 0.01 us
  starting transfers between devices: 33.9 us -> 32.5 us
  Pallas kernels: 10.5 us -> 11.6 us
    ppermute x4 -> x3, starting transfers between devices: 27 us -> 15.6 us  [moved(): return lax.ppermute(value, 'seq', [(s, s + by) for s in range(count - by)])]
    ppermute x0 -> x1, starting transfers between devices: none -> 9.97 us  [local(): lax.ppermute(joined, 'seq', [(s, (s ^ 2) + 16) for s in range(count - 16)])]
    unnamed x12 -> x0, local copies, waits for them, and re-layouts: 4.4 us -> none
    pallas_call x8, Pallas kernels: 10.5 us -> 11.6 us  [call(): pl.pallas_call(kernel, out_shape=outs if len(outs) > 1 else outs[0], in_s...]
    ppermute x4 -> x3, waiting for transfers between devices: 4.97 us -> 5.45 us  [moved(): return lax.ppermute(value, 'seq', [(s, s + by) for s in range(count - by)])]
where the time goes in v2:
time: 84.9 us; the launch traced here: 84.6 us
  starting transfers between devices  32.5 us (38%)
  blocking collectives  29.9 us (35%)
  Pallas kernels  11.6 us (14%)
  waiting for transfers between devices  10.5 us (12%)
    all_to_all x1, blocking collectives, local(): received = lax.all_to_all(packed, 'head', 0, 0, tiled=True)  19.2 us
    ppermute x3, starting transfers between devices, moved(): return lax.ppermute(value, 'seq', [(s, s + by) for s in range(count - by)])  15.6 us
    pallas_call x8, Pallas kernels, call(): pl.pallas_call(kernel, out_shape=outs if len(outs) > 1 else outs[0], in_s...  11.6 us
    all_to_all x1, blocking collectives, local(): lax.all_to_all(normed.reshape(HEADS, TOK, D), 'head', 0, 0, tiled=True)  10.7 us
    ppermute x1, starting transfers between devices, local(): lax.ppermute(joined, 'seq', [(s, (s ^ 2) + 16) for s in range(count - 16)])  9.97 us
    all_to_all x1, starting transfers between devices, local(): lax.all_to_all(maps, 'seq', 0, 0, axis_index_groups=groups, tiled=True)  6.9 us
    ppermute x3, waiting for transfers between devices, moved(): return lax.ppermute(value, 'seq', [(s, s + by) for s in range(count - by)])  5.45 us
    all_to_all x1, waiting for transfers between devices, local(): lax.all_to_all(maps, 'seq', 0, 0, axis_index_groups=groups, tiled=True)  5.04 us
  transfers between devices with their start and end apart: 5, of which 2 were waited for; matrix products, arithmetic and copies ran while one was open for 0% of the time, Pallas kernels for 3%

profile of v2, /device:TPU:1, one launch (start us, length us, event | category | flops | bytes accessed | tf_op | source)
XLA Modules:
  0.0 84.6 jit_solution(12202534291736607523)
XLA Ops:
  0.0 1.8 %shard_map.64 = (bf16[16,200,128]{2,1,0:T(8,128)(2,1)S(1)}, f32[1,128]{1,0:T(1,128)S(1)}) custom-call(bf16[16,64]{1,0:T(8,128)(2,1)} %bitcast.6, bf16[16,64]{1,0:T(8,128)(2,1)} %bitcast.7, f32[1,128]{1,0:T(1,128)} %bitcast.8, bf16[64,16,128]{2,1,0:T(8,128)(2,1)} %refs_3_.1, bf16[64,16,128]{2,1,0:T(8,128)(2,1)} %refs_4_.1, bf16[64,16,128]{2,1,0:T(8,128)(2,1)} %refs_5_.1), custom_call_target="tpu_custom_call" | custom-call | bytes 791040 | tf_op jit(solution)/shard_map/pallas_call | solution.py:254
  1.8 19.2 %all_to_all.15.received = bf16[16,200,128]{2,1,0:T(8,128)(2,1)S(1)} all-to-all(bf16[16,200,128]{2,1,0:T(8,128)(2,1)S(1)} %get-tuple-element.16), channel_id=1, replica_groups=mesh['seq'=32,'head'=16] {'head'}, dimensions={0} | all-to-all | bytes 1638400 | tf_op jit(solution)/shard_map/all_to_all | solution.py:282
  21.0 5.2 %shard_map.65 = (bf16[4,128,256]{2,1,0:T(8,128)(2,1)}, f32[8,128,256]{2,1,0:T(8,128)S(1)}, f32[8,128,256]{2,1,0:T(8,128)S(1)}) custom-call(bf16[16,200,128]{2,1,0:T(8,128)(2,1)S(1)} %all_to_all.15.received), custom_call_target="tpu_custom_call" | custom-call | flops 8589934592 | bytes 819200 | tf_op jit(solution)/shard_map/pallas_call | solution.py:254
  26.2 6.9 %all-to-all-start.1 = ((bf16[4,128,256]{2,1,0:T(8,128)(2,1)}), bf16[4,128,256]{2,1,0:T(8,128)(2,1)S(1)}, u32[]{:S(2)}, u32[]{:S(2)}) async-start(bf16[4,128,256]{2,1,0:T(8,128)(2,1)} %get-tuple-element.17), calls=%async_computation.1 | async-start | bytes 524288 | tf_op jit(solution)/shard_map/all_to_all | solution.py:291
  33.1 5.0 %all-to-all-done.1.received = bf16[4,128,256]{2,1,0:T(8,128)(2,1)S(1)} async-done(((bf16[4,128,256]{2,1,0:T(8,128)(2,1)}), bf16[4,128,256]{2,1,0:T(8,128)(2,1)S(1)}, u32[]{:S(2)}, u32[]{:S(2)}) %all-to-all-start.1) | async-done | bytes 262176 | tf_op jit(solution)/shard_map/all_to_all | solution.py:291
  38.1 0.5 shard_map.66
  38.6 4.9 %collective-permute-start = (bf16[128,256]{1,0:T(8,128)(2,1)S(1)}, bf16[128,256]{1,0:T(8,128)(2,1)S(1)}, u32[]{:S(2)}, u32[]{:S(2)}) collective-permute-start(bf16[128,256]{1,0:T(8,128)(2,1)S(1)} %get-tuple-element.18.total), channel_id=1, source_target_pairs={{0,64},{16,80},{32,96},{48,112},{64,128},{80,144},{96,160},{112,17... | collective-permute-start | bytes 196616 | tf_op jit(solution)/shard_map/ppermute | solution.py:306
  43.5 1.6 %shard_map.68 = (bf16[1024,256]{1,0:T(8,128)(2,1)S(1)}, f32[1024,128]{1,0:T(8,128)S(1)}) custom-call(bf16[16,200,128]{2,1,0:T(8,128)(2,1)S(1)} %all_to_all.15.received, f32[8,128,256]{2,1,0:T(8,128)S(1)} %get-tuple-element.20.prefixes, f32[8,128,256]{2,1,0:T(8,128)S(1)} %get-tuple-element.21.solved), custom_call_target="tpu_custom_call" | custom-call | flops 8589934592 | bytes 2916352 | tf_op jit(solution)/shard_map/pallas_call | solution.py:254
  45.2 0.0 collective-permute-done.earlier
  45.2 0.1 shard_map.67
  45.4 9.4 %collective-permute-start.1 = (bf16[128,256]{1,0:T(8,128)(2,1)S(1)}, bf16[128,256]{1,0:T(8,128)(2,1)S(1)}, u32[]{:S(2)}, u32[]{:S(2)}) collective-permute-start(bf16[128,256]{1,0:T(8,128)(2,1)S(1)} %shard_map.67), channel_id=1, source_target_pairs={{0,128},{16,144},{32,160},{48,176},{64,192},{80,208},{96,224},{112... | collective-permute-start | bytes 196616 | tf_op jit(solution)/shard_map/ppermute | solution.py:306
  54.8 10.0 %collective-permute-start.2 = (bf16[128,256]{1,0:T(8,128)(2,1)S(1)}, bf16[128,256]{1,0:T(8,128)(2,1)S(1)}, u32[]{:S(2)}, u32[]{:S(2)}) collective-permute-start(bf16[128,256]{1,0:T(8,128)(2,1)S(1)} %shard_map.67), channel_id=1, source_target_pairs={{0,288},{16,304},{32,256},{48,272},{64,352},{80,368},{96,320},{112... | collective-permute-start | bytes 196616 | tf_op jit(solution)/shard_map/ppermute | solution.py:311
  64.8 1.3 %collective-permute-start.3 = (bf16[128,128]{1,0:T(8,128)(2,1)S(1)}, bf16[128,128]{1,0:T(8,128)(2,1)S(1)}, u32[]{:S(2)}, u32[]{:S(2)}) collective-permute-start(bf16[128,128]{1,0:T(8,128)(2,1)S(1)} %slice.4), channel_id=1, source_target_pairs={{0,384},{16,400},{32,416},{48,432},{64,448},{80,464},{96,480},{112... | collective-permute-start | bytes 98312 | tf_op jit(solution)/shard_map/ppermute | solution.py:306
  66.1 0.6 shard_map.69
  66.7 5.4 %collective-permute-done.3.farthest = bf16[128,128]{1,0:T(8,128)(2,1)S(1)} collective-permute-done((bf16[128,128]{1,0:T(8,128)(2,1)S(1)}, bf16[128,128]{1,0:T(8,128)(2,1)S(1)}, u32[]{:S(2)}, u32[]{:S(2)}) %collective-permute-start.3) | collective-permute-done | bytes 32800 | tf_op jit(solution)/shard_map/ppermute | solution.py:306
  72.1 0.0 collective-permute-done.1.near
  72.1 0.0 collective-permute-done.2.far
  72.1 0.7 shard_map.70
  72.9 10.7 %all_to_all.16.received = bf16[16,64,128]{2,1,0:T(8,128)(2,1)S(1)} all-to-all(bf16[16,64,128]{2,1,0:T(8,128)(2,1)S(1)} %bitcast.5), channel_id=1, replica_groups=mesh['seq'=32,'head'=16] {'head'}, dimensions={0} | all-to-all | bytes 524288 | tf_op jit(solution)/shard_map/all_to_all | solution.py:332
  83.5 1.0 %shard_map.71 = bf16[64,16,128]{2,1,0:T(8,128)(2,1)} custom-call(bf16[16,64,128]{2,1,0:T(8,128)(2,1)S(1)} %all_to_all.16.received), custom_call_target="tpu_custom_call" | custom-call | bytes 262144 | tf_op jit(solution)/shard_map/pallas_call | solution.py:254
  (1 shorter events, 0.0 us)
Async XLA Ops:
  26.2 11.9 %all-to-all-start.1 = ((bf16[4,128,256]{2,1,0:T(8,128)(2,1)}), bf16[4,128,256]{2,1,0:T(8,128)(2,1)S(1)}, u32[]{:S(2)}, u32[]{:S(2)}) async-start(bf16[4,128,256]{2,1,0:T(8,128)(2,1)} %get-tuple-element.17), calls=%async_computation.1 | async-start | bytes 524288 | tf_op jit(solution)/shard_map/all_to_all | solution.py:291
  38.6 6.6 %collective-permute-start = (bf16[128,256]{1,0:T(8,128)(2,1)S(1)}, bf16[128,256]{1,0:T(8,128)(2,1)S(1)}, u32[]{:S(2)}, u32[]{:S(2)}) collective-permute-start(bf16[128,256]{1,0:T(8,128)(2,1)S(1)} %get-tuple-element.18.total), channel_id=1, source_target_pairs={{0,64},{16,80},{32,96},{48,112},{64,128},{80,144},{96,160},{112,17... | collective-permute-start | bytes 196616 | tf_op jit(solution)/shard_map/ppermute | solution.py:306
  45.4 26.8 %collective-permute-start.1 = (bf16[128,256]{1,0:T(8,128)(2,1)S(1)}, bf16[128,256]{1,0:T(8,128)(2,1)S(1)}, u32[]{:S(2)}, u32[]{:S(2)}) collective-permute-start(bf16[128,256]{1,0:T(8,128)(2,1)S(1)} %shard_map.67), channel_id=1, source_target_pairs={{0,128},{16,144},{32,160},{48,176},{64,192},{80,208},{96,224},{112... | collective-permute-start | bytes 196616 | tf_op jit(solution)/shard_map/ppermute | solution.py:306
  54.8 17.4 %collective-permute-start.2 = (bf16[128,256]{1,0:T(8,128)(2,1)S(1)}, bf16[128,256]{1,0:T(8,128)(2,1)S(1)}, u32[]{:S(2)}, u32[]{:S(2)}) collective-permute-start(bf16[128,256]{1,0:T(8,128)(2,1)S(1)} %shard_map.67), channel_id=1, source_target_pairs={{0,288},{16,304},{32,256},{48,272},{64,352},{80,368},{96,320},{112... | collective-permute-start | bytes 196616 | tf_op jit(solution)/shard_map/ppermute | solution.py:311
  64.8 7.4 %collective-permute-start.3 = (bf16[128,128]{1,0:T(8,128)(2,1)S(1)}, bf16[128,128]{1,0:T(8,128)(2,1)S(1)}, u32[]{:S(2)}, u32[]{:S(2)}) collective-permute-start(bf16[128,128]{1,0:T(8,128)(2,1)S(1)} %slice.4), channel_id=1, source_target_pairs={{0,384},{16,400},{32,416},{48,432},{64,448},{80,464},{96,480},{112... | collective-permute-start | bytes 98312 | tf_op jit(solution)/shard_map/ppermute | solution.py:306

commit v3 on v2

--- a/solution.py
+++ b/solution.py
@@ -170,8 +170,7 @@
             prefixes[c] = prefix
             moved = mm3_wide(linear, prefix)
             prefix = jnp.concatenate([moved[:, :D], moved[:, D:] + offset], axis=1)
-    for copy in range(4):
-        sent[copy] = prefix.astype(BF16)
+    sent[...] = prefix.astype(BF16)
 
 
 def query_kernel(received, prefixes, solved, query_maps, base):
@@ -193,19 +192,24 @@
         base[c * CHUNK : (c + 1) * CHUNK, :] = result[:, D:]
 
 
-def block_kernel(place, received, before, total):
+def block_kernel(place, own, next_core, next_chip, across, before, total):
+    odd, upper = place[0] % 2 == 1, place[0] >= 2
+    low = jnp.where(odd, next_core[...], own[...]), jnp.where(odd, own[...], next_core[...])
+    high = jnp.where(odd, across[...], next_chip[...]), jnp.where(odd, next_chip[...], across[...])
+    block = [jnp.where(upper, b, a) for a, b in zip(low, high)]
+    block += [jnp.where(upper, a, b) for a, b in zip(low, high)]
     eye = jnp.where(jnp.equal(*iotas(D, D)), 1.0, 0.0)
     prefix = jnp.concatenate([eye, jnp.zeros_like(eye)], axis=1)
     chosen = prefix
     for p in range(4):
         if p:
             chosen = jnp.where(place[0] == p, prefix, chosen)
-        linear = received[p, :, :D]
+        linear = block[p][:, :D]
         if p == 0:
-            prefix = received[p].astype(F32)
+            prefix = block[p].astype(F32)
         else:
             moved = mm(twice(linear, 1), tall(prefix))
-            offset = received[p, :, D:].astype(F32)
+            offset = block[p][:, D:].astype(F32)
             prefix = jnp.concatenate([moved[:, :D], moved[:, D:] + offset], axis=1)
     before[...] = chosen
     total[...] = prefix.astype(BF16)
@@ -282,13 +286,16 @@
     received = lax.all_to_all(packed, "head", 0, 0, tiled=True)
     maps, prefixes, solved = call(
         map_kernel,
-        [((4, D, 2 * D), BF16), ((CHUNKS, D, 2 * D), F32), ((CHUNKS, CHUNK, 2 * D), F32)],
+        [((D, 2 * D), BF16), ((CHUNKS, D, 2 * D), F32), ((CHUNKS, CHUNK, 2 * D), F32)],
         received,
         flops=1 << 33,
     )
     count = lax.axis_size("seq")
-    groups = [[first + p for p in range(4)] for first in range(0, count, 4)]
-    block = lax.all_to_all(maps, "seq", 0, 0, axis_index_groups=groups, tiled=True)
+
+    def swapped(bits):
+        return lax.ppermute(maps, "seq", [(s, s ^ bits) for s in range(count)])
+
+    block = [maps, swapped(1), swapped(2), swapped(3)]
     query_maps, base = call(
         query_kernel,
         [((SLAB, 2 * D), BF16), ((SLAB, D), F32)],
@@ -299,7 +306,7 @@
     )
     place = (lax.axis_index("seq") % 4).astype(jnp.int32).reshape(1)
     before, total = call(
-        block_kernel, [((D, 2 * D), F32), ((D, 2 * D), BF16)], place, block, scalars=1
+        block_kernel, [((D, 2 * D), F32), ((D, 2 * D), BF16)], place, *block, scalars=1
     )
 
     def moved(value, by):

time: 84.9 us -> 82.3 us (0.969)
  waiting for transfers between devices: 10.5 us -> 2.8 us
  starting transfers between devices: 32.5 us -> 37.7 us
    ppermute x0 -> x3, starting transfers between devices: none -> 11.2 us  [swapped(): return lax.ppermute(maps, 'seq', [(s, s ^ bits) for s in range(count)])]
    all_to_all x1 -> x0, starting transfers between devices: 6.9 us -> none  [local(): lax.all_to_all(maps, 'seq', 0, 0, axis_index_groups=groups, tiled=True)]
    ppermute x1, starting transfers between devices: 9.97 us -> 16.1 us  [local(): lax.ppermute(joined, 'seq', [(s, (s ^ 2) + 16) for s in range(count - 16)])]
    ppermute x3, starting transfers between devices: 15.6 us -> 10.5 us  [moved(): return lax.ppermute(value, 'seq', [(s, s + by) for s in range(count - by)])]
    all_to_all x1 -> x0, waiting for transfers between devices: 5.04 us -> none  [local(): lax.all_to_all(maps, 'seq', 0, 0, axis_index_groups=groups, tiled=True)]
    ppermute x3, waiting for transfers between devices: 5.45 us -> 1.94 us  [moved(): return lax.ppermute(value, 'seq', [(s, s + by) for s in range(count - by)])]
    ppermute x0 -> x3, waiting for transfers between devices: none -> 0.86 us  [swapped(): return lax.ppermute(maps, 'seq', [(s, s ^ bits) for s in range(count)])]
  transfers between devices with their start and end apart: 5 -> 7, of which waited for: 2 -> 3; matrix products, arithmetic and copies ran while one was open for 0% -> 0% of each run, Pallas kernels for 3% -> 3%
where the time goes in v3:
time: 82.3 us; the launch traced here: 81.3 us
  starting transfers between devices  37.7 us (46%)
  blocking collectives  29.8 us (36%)
  Pallas kernels  10.9 us (13%)
  waiting for transfers between devices  2.8 us (3%)
    all_to_all x1, blocking collectives, local(): received = lax.all_to_all(packed, 'head', 0, 0, tiled=True)  19.2 us
    ppermute x1, starting transfers between devices, local(): lax.ppermute(joined, 'seq', [(s, (s ^ 2) + 16) for s in range(count - 16)])  16.1 us
    ppermute x3, starting transfers between devices, swapped(): return lax.ppermute(maps, 'seq', [(s, s ^ bits) for s in range(count)])  11.2 us
    pallas_call x8, Pallas kernels, call(): pl.pallas_call(kernel, out_shape=outs if len(outs) > 1 else outs[0], in_s...  10.9 us
    all_to_all x1, blocking collectives, local(): lax.all_to_all(normed.reshape(HEADS, TOK, D), 'head', 0, 0, tiled=True)  10.6 us
    ppermute x3, starting transfers between devices, moved(): return lax.ppermute(value, 'seq', [(s, s + by) for s in range(count - by)])  10.5 us
    ppermute x3, waiting for transfers between devices, moved(): return lax.ppermute(value, 'seq', [(s, s + by) for s in range(count - by)])  1.94 us
  transfers between devices with their start and end apart: 7, of which 3 were waited for; matrix products, arithmetic and copies ran while one was open for 0% of the time, Pallas kernels for 3%

profile of v3, /device:TPU:1, one launch (start us, length us, event | category | flops | bytes accessed | tf_op | source)
XLA Modules:
  0.0 81.3 jit_solution(14118056953365033616)
XLA Ops:
  0.0 1.8 %shard_map.64 = (bf16[16,200,128]{2,1,0:T(8,128)(2,1)S(1)}, f32[1,128]{1,0:T(1,128)S(1)}) custom-call(bf16[16,64]{1,0:T(8,128)(2,1)} %bitcast.6, bf16[16,64]{1,0:T(8,128)(2,1)} %bitcast.7, f32[1,128]{1,0:T(1,128)} %bitcast.8, bf16[64,16,128]{2,1,0:T(8,128)(2,1)} %refs_3_.1, bf16[64,16,128]{2,1,0:T(8,128)(2,1)} %refs_4_.1, bf16[64,16,128]{2,1,0:T(8,128)(2,1)} %refs_5_.1), custom_call_target="tpu_custom_call" | custom-call | bytes 791040 | tf_op jit(solution)/shard_map/pallas_call | solution.py:258
  1.8 19.2 %all_to_all.10.received = bf16[16,200,128]{2,1,0:T(8,128)(2,1)S(1)} all-to-all(bf16[16,200,128]{2,1,0:T(8,128)(2,1)S(1)} %get-tuple-element.16), channel_id=1, replica_groups=mesh['seq'=32,'head'=16] {'head'}, dimensions={0} | all-to-all | bytes 1638400 | tf_op jit(solution)/shard_map/all_to_all | solution.py:286
  21.0 4.5 %shard_map.65 = (bf16[128,256]{1,0:T(8,128)(2,1)S(1)}, f32[8,128,256]{2,1,0:T(8,128)S(1)}, f32[8,128,256]{2,1,0:T(8,128)S(1)}) custom-call(bf16[16,200,128]{2,1,0:T(8,128)(2,1)S(1)} %all_to_all.10.received), custom_call_target="tpu_custom_call" | custom-call | flops 8589934592 | bytes 819200 | tf_op jit(solution)/shard_map/pallas_call | solution.py:258
  25.5 7.0 %collective-permute-start.2 = (bf16[128,256]{1,0:T(8,128)(2,1)S(1)}, bf16[128,256]{1,0:T(8,128)(2,1)S(1)}, u32[]{:S(2)}, u32[]{:S(2)}) collective-permute-start(bf16[128,256]{1,0:T(8,128)(2,1)S(1)} %get-tuple-element.17.own), channel_id=1, source_target_pairs={{0,48},{16,32},{32,16},{48,0},{64,112},{80,96},{96,80},{112,64},{1... | collective-permute-start | bytes 196616 | tf_op jit(solution)/shard_map/ppermute | solution.py:296
  32.5 1.9 %collective-permute-start.1 = (bf16[128,256]{1,0:T(8,128)(2,1)S(1)}, bf16[128,256]{1,0:T(8,128)(2,1)S(1)}, u32[]{:S(2)}, u32[]{:S(2)}) collective-permute-start(bf16[128,256]{1,0:T(8,128)(2,1)S(1)} %get-tuple-element.17.own), channel_id=1, source_target_pairs={{0,32},{16,48},{32,0},{48,16},{64,96},{80,112},{96,64},{112,80},{1... | collective-permute-start | bytes 196616 | tf_op jit(solution)/shard_map/ppermute | solution.py:296
  34.4 2.3 %collective-permute-start = (bf16[128,256]{1,0:T(8,128)(2,1)S(1)}, bf16[128,256]{1,0:T(8,128)(2,1)S(1)}, u32[]{:S(2)}, u32[]{:S(2)}) collective-permute-start(bf16[128,256]{1,0:T(8,128)(2,1)S(1)} %get-tuple-element.17.own), channel_id=1, source_target_pairs={{0,16},{16,0},{32,48},{48,32},{64,80},{80,64},{96,112},{112,96},{1... | collective-permute-start | bytes 196616 | tf_op jit(solution)/shard_map/ppermute | solution.py:296
  36.7 0.0 collective-permute-done.2.across
  36.7 0.7 collective-permute-done.1.next_chip
  37.5 0.1 collective-permute-done.next_core
  37.6 0.5 shard_map.66
  38.1 4.9 %collective-permute-start.3 = (bf16[128,256]{1,0:T(8,128)(2,1)S(1)}, bf16[128,256]{1,0:T(8,128)(2,1)S(1)}, u32[]{:S(2)}, u32[]{:S(2)}) collective-permute-start(bf16[128,256]{1,0:T(8,128)(2,1)S(1)} %get-tuple-element.18.total), channel_id=1, source_target_pairs={{0,64},{16,80},{32,96},{48,112},{64,128},{80,144},{96,160},{112,17... | collective-permute-start | bytes 196616 | tf_op jit(solution)/shard_map/ppermute | solution.py:313
  43.0 1.6 %shard_map.68 = (bf16[1024,256]{1,0:T(8,128)(2,1)S(1)}, f32[1024,128]{1,0:T(8,128)S(1)}) custom-call(bf16[16,200,128]{2,1,0:T(8,128)(2,1)S(1)} %all_to_all.10.received, f32[8,128,256]{2,1,0:T(8,128)S(1)} %get-tuple-element.20.prefixes, f32[8,128,256]{2,1,0:T(8,128)S(1)} %get-tuple-element.21.solved), custom_call_target="tpu_custom_call" | custom-call | flops 8589934592 | bytes 2916352 | tf_op jit(solution)/shard_map/pallas_call | solution.py:258
  44.6 0.0 collective-permute-done.3.earlier
  44.6 0.1 shard_map.67
  44.8 16.1 %collective-permute-start.5 = (bf16[128,256]{1,0:T(8,128)(2,1)S(1)}, bf16[128,256]{1,0:T(8,128)(2,1)S(1)}, u32[]{:S(2)}, u32[]{:S(2)}) collective-permute-start(bf16[128,256]{1,0:T(8,128)(2,1)S(1)} %shard_map.67), channel_id=1, source_target_pairs={{0,288},{16,304},{32,256},{48,272},{64,352},{80,368},{96,320},{112... | collective-permute-start | bytes 196616 | tf_op jit(solution)/shard_map/ppermute | solution.py:318
  60.9 4.3 %collective-permute-start.4 = (bf16[128,256]{1,0:T(8,128)(2,1)S(1)}, bf16[128,256]{1,0:T(8,128)(2,1)S(1)}, u32[]{:S(2)}, u32[]{:S(2)}) collective-permute-start(bf16[128,256]{1,0:T(8,128)(2,1)S(1)} %shard_map.67), channel_id=1, source_target_pairs={{0,128},{16,144},{32,160},{48,176},{64,192},{80,208},{96,224},{112... | collective-permute-start | bytes 196616 | tf_op jit(solution)/shard_map/ppermute | solution.py:313
  65.2 1.3 %collective-permute-start.6 = (bf16[128,128]{1,0:T(8,128)(2,1)S(1)}, bf16[128,128]{1,0:T(8,128)(2,1)S(1)}, u32[]{:S(2)}, u32[]{:S(2)}) collective-permute-start(bf16[128,128]{1,0:T(8,128)(2,1)S(1)} %slice.4), channel_id=1, source_target_pairs={{0,384},{16,400},{32,416},{48,432},{64,448},{80,464},{96,480},{112... | collective-permute-start | bytes 98312 | tf_op jit(solution)/shard_map/ppermute | solution.py:313
  66.5 0.6 shard_map.69
  67.1 1.9 %collective-permute-done.6.farthest = bf16[128,128]{1,0:T(8,128)(2,1)S(1)} collective-permute-done((bf16[128,128]{1,0:T(8,128)(2,1)S(1)}, bf16[128,128]{1,0:T(8,128)(2,1)S(1)}, u32[]{:S(2)}, u32[]{:S(2)}) %collective-permute-start.6) | collective-permute-done | bytes 32800 | tf_op jit(solution)/shard_map/ppermute | solution.py:313
  69.0 0.0 collective-permute-done.5.far
  69.0 0.0 collective-permute-done.4.near
  69.0 0.7 shard_map.70
  69.7 10.6 %all_to_all.11.received = bf16[16,64,128]{2,1,0:T(8,128)(2,1)S(1)} all-to-all(bf16[16,64,128]{2,1,0:T(8,128)(2,1)S(1)} %bitcast.5), channel_id=1, replica_groups=mesh['seq'=32,'head'=16] {'head'}, dimensions={0} | all-to-all | bytes 524288 | tf_op jit(solution)/shard_map/all_to_all | solution.py:339
  80.3 1.0 %shard_map.71 = bf16[64,16,128]{2,1,0:T(8,128)(2,1)} custom-call(bf16[16,64,128]{2,1,0:T(8,128)(2,1)S(1)} %all_to_all.11.received), custom_call_target="tpu_custom_call" | custom-call | bytes 262144 | tf_op jit(solution)/shard_map/pallas_call | solution.py:258
  (1 shorter events, 0.0 us)
Async XLA Ops:
  25.5 11.2 %collective-permute-start.2 = (bf16[128,256]{1,0:T(8,128)(2,1)S(1)}, bf16[128,256]{1,0:T(8,128)(2,1)S(1)}, u32[]{:S(2)}, u32[]{:S(2)}) collective-permute-start(bf16[128,256]{1,0:T(8,128)(2,1)S(1)} %get-tuple-element.17.own), channel_id=1, source_target_pairs={{0,48},{16,32},{32,16},{48,0},{64,112},{80,96},{96,80},{112,64},{1... | collective-permute-start | bytes 196616 | tf_op jit(solution)/shard_map/ppermute | solution.py:296
  32.5 5.0 %collective-permute-start.1 = (bf16[128,256]{1,0:T(8,128)(2,1)S(1)}, bf16[128,256]{1,0:T(8,128)(2,1)S(1)}, u32[]{:S(2)}, u32[]{:S(2)}) collective-permute-start(bf16[128,256]{1,0:T(8,128)(2,1)S(1)} %get-tuple-element.17.own), channel_id=1, source_target_pairs={{0,32},{16,48},{32,0},{48,16},{64,96},{80,112},{96,64},{112,80},{1... | collective-permute-start | bytes 196616 | tf_op jit(solution)/shard_map/ppermute | solution.py:296
  34.4 3.2 %collective-permute-start = (bf16[128,256]{1,0:T(8,128)(2,1)S(1)}, bf16[128,256]{1,0:T(8,128)(2,1)S(1)}, u32[]{:S(2)}, u32[]{:S(2)}) collective-permute-start(bf16[128,256]{1,0:T(8,128)(2,1)S(1)} %get-tuple-element.17.own), channel_id=1, source_target_pairs={{0,16},{16,0},{32,48},{48,32},{64,80},{80,64},{96,112},{112,96},{1... | collective-permute-start | bytes 196616 | tf_op jit(solution)/shard_map/ppermute | solution.py:296
  38.1 6.6 %collective-permute-start.3 = (bf16[128,256]{1,0:T(8,128)(2,1)S(1)}, bf16[128,256]{1,0:T(8,128)(2,1)S(1)}, u32[]{:S(2)}, u32[]{:S(2)}) collective-permute-start(bf16[128,256]{1,0:T(8,128)(2,1)S(1)} %get-tuple-element.18.total), channel_id=1, source_target_pairs={{0,64},{16,80},{32,96},{48,112},{64,128},{80,144},{96,160},{112,17... | collective-permute-start | bytes 196616 | tf_op jit(solution)/shard_map/ppermute | solution.py:313
  44.8 24.2 %collective-permute-start.5 = (bf16[128,256]{1,0:T(8,128)(2,1)S(1)}, bf16[128,256]{1,0:T(8,128)(2,1)S(1)}, u32[]{:S(2)}, u32[]{:S(2)}) collective-permute-start(bf16[128,256]{1,0:T(8,128)(2,1)S(1)} %shard_map.67), channel_id=1, source_target_pairs={{0,288},{16,304},{32,256},{48,272},{64,352},{80,368},{96,320},{112... | collective-permute-start | bytes 196616 | tf_op jit(solution)/shard_map/ppermute | solution.py:318
  60.9 8.2 %collective-permute-start.4 = (bf16[128,256]{1,0:T(8,128)(2,1)S(1)}, bf16[128,256]{1,0:T(8,128)(2,1)S(1)}, u32[]{:S(2)}, u32[]{:S(2)}) collective-permute-start(bf16[128,256]{1,0:T(8,128)(2,1)S(1)} %shard_map.67), channel_id=1, source_target_pairs={{0,128},{16,144},{32,160},{48,176},{64,192},{80,208},{96,224},{112... | collective-permute-start | bytes 196616 | tf_op jit(solution)/shard_map/ppermute | solution.py:313
  65.2 3.9 %collective-permute-start.6 = (bf16[128,128]{1,0:T(8,128)(2,1)S(1)}, bf16[128,128]{1,0:T(8,128)(2,1)S(1)}, u32[]{:S(2)}, u32[]{:S(2)}) collective-permute-start(bf16[128,128]{1,0:T(8,128)(2,1)S(1)} %slice.4), channel_id=1, source_target_pairs={{0,384},{16,400},{32,416},{48,432},{64,448},{80,464},{96,480},{112... | collective-permute-start | bytes 98312 | tf_op jit(solution)/shard_map/ppermute | solution.py:313

commit v4 on v3

--- a/solution.py
+++ b/solution.py
@@ -147,8 +147,13 @@
         mask = (apart >> level) == 1
         for c in range(CHUNKS):
             inverse = inverses[c]
-            inner = mm3(inverse, jnp.where(mask, lowers[c], 0.0))
-            inverses[c] = inverse - mm3(inner, inverse)
+            lower = jnp.where(mask, lowers[c], 0.0)
+            if level < 4:
+                inverse = inverse.astype(BF16)
+                inner = mm(inverse, lower.astype(BF16)).astype(BF16)
+                inverses[c] = inverses[c] - mm(inner, inverse)
+            else:
+                inverses[c] = inverse - mm3(mm3(inverse, lower), inverse)
     log_scale = jnp.exp(log_rows)
     prefix = None
     for c in range(CHUNKS):

time: 82.3 us -> 82.2 us (level)
  no operation moved by 1% of the time
where the time goes in v4:
time: 82.2 us; the launch traced here: 81.2 us
  starting transfers between devices  37.7 us (46%)
  blocking collectives  29.8 us (36%)
  Pallas kernels  10.7 us (13%)
  waiting for transfers between devices  2.8 us (3%)
    all_to_all x1, blocking collectives, local(): received = lax.all_to_all(packed, 'head', 0, 0, tiled=True)  19.2 us
    ppermute x1, starting transfers between devices, local(): lax.ppermute(joined, 'seq', [(s, (s ^ 2) + 16) for s in range(count - 16)])  16.1 us
    ppermute x3, starting transfers between devices, swapped(): return lax.ppermute(maps, 'seq', [(s, s ^ bits) for s in range(count)])  11.2 us
    pallas_call x8, Pallas kernels, call(): pl.pallas_call(kernel, out_shape=outs if len(outs) > 1 else outs[0], in_s...  10.7 us
    all_to_all x1, blocking collectives, local(): lax.all_to_all(normed.reshape(HEADS, TOK, D), 'head', 0, 0, tiled=True)  10.6 us
    ppermute x3, starting transfers between devices, moved(): return lax.ppermute(value, 'seq', [(s, s + by) for s in range(count - by)])  10.5 us
    ppermute x3, waiting for transfers between devices, moved(): return lax.ppermute(value, 'seq', [(s, s + by) for s in range(count - by)])  1.94 us
  transfers between devices with their start and end apart: 7, of which 3 were waited for; matrix products, arithmetic and copies ran while one was open for 0% of the time, Pallas kernels for 3%

profile of v4, /device:TPU:1, one launch (start us, length us, event | category | flops | bytes accessed | tf_op | source)
XLA Modules:
  0.0 81.2 jit_solution(11976018937574819356)
XLA Ops:
  0.0 1.8 %shard_map.64 = (bf16[16,200,128]{2,1,0:T(8,128)(2,1)S(1)}, f32[1,128]{1,0:T(1,128)S(1)}) custom-call(bf16[16,64]{1,0:T(8,128)(2,1)} %bitcast.6, bf16[16,64]{1,0:T(8,128)(2,1)} %bitcast.7, f32[1,128]{1,0:T(1,128)} %bitcast.8, bf16[64,16,128]{2,1,0:T(8,128)(2,1)} %refs_3_.1, bf16[64,16,128]{2,1,0:T(8,128)(2,1)} %refs_4_.1, bf16[64,16,128]{2,1,0:T(8,128)(2,1)} %refs_5_.1), custom_call_target="tpu_custom_call" | custom-call | bytes 791040 | tf_op jit(solution)/shard_map/pallas_call | solution.py:263
  1.8 19.2 %all_to_all.10.received = bf16[16,200,128]{2,1,0:T(8,128)(2,1)S(1)} all-to-all(bf16[16,200,128]{2,1,0:T(8,128)(2,1)S(1)} %get-tuple-element.16), channel_id=1, replica_groups=mesh['seq'=32,'head'=16] {'head'}, dimensions={0} | all-to-all | bytes 1638400 | tf_op jit(solution)/shard_map/all_to_all | solution.py:291
  21.0 4.3 %shard_map.65 = (bf16[128,256]{1,0:T(8,128)(2,1)S(1)}, f32[8,128,256]{2,1,0:T(8,128)S(1)}, f32[8,128,256]{2,1,0:T(8,128)S(1)}) custom-call(bf16[16,200,128]{2,1,0:T(8,128)(2,1)S(1)} %all_to_all.10.received), custom_call_target="tpu_custom_call" | custom-call | flops 8589934592 | bytes 819200 | tf_op jit(solution)/shard_map/pallas_call | solution.py:263
  25.4 7.0 %collective-permute-start.2 = (bf16[128,256]{1,0:T(8,128)(2,1)S(1)}, bf16[128,256]{1,0:T(8,128)(2,1)S(1)}, u32[]{:S(2)}, u32[]{:S(2)}) collective-permute-start(bf16[128,256]{1,0:T(8,128)(2,1)S(1)} %get-tuple-element.17.own), channel_id=1, source_target_pairs={{0,48},{16,32},{32,16},{48,0},{64,112},{80,96},{96,80},{112,64},{1... | collective-permute-start | bytes 196616 | tf_op jit(solution)/shard_map/ppermute | solution.py:301
  32.3 1.9 %collective-permute-start.1 = (bf16[128,256]{1,0:T(8,128)(2,1)S(1)}, bf16[128,256]{1,0:T(8,128)(2,1)S(1)}, u32[]{:S(2)}, u32[]{:S(2)}) collective-permute-start(bf16[128,256]{1,0:T(8,128)(2,1)S(1)} %get-tuple-element.17.own), channel_id=1, source_target_pairs={{0,32},{16,48},{32,0},{48,16},{64,96},{80,112},{96,64},{112,80},{1... | collective-permute-start | bytes 196616 | tf_op jit(solution)/shard_map/ppermute | solution.py:301
  34.3 2.3 %collective-permute-start = (bf16[128,256]{1,0:T(8,128)(2,1)S(1)}, bf16[128,256]{1,0:T(8,128)(2,1)S(1)}, u32[]{:S(2)}, u32[]{:S(2)}) collective-permute-start(bf16[128,256]{1,0:T(8,128)(2,1)S(1)} %get-tuple-element.17.own), channel_id=1, source_target_pairs={{0,16},{16,0},{32,48},{48,32},{64,80},{80,64},{96,112},{112,96},{1... | collective-permute-start | bytes 196616 | tf_op jit(solution)/shard_map/ppermute | solution.py:301
  36.6 0.0 collective-permute-done.2.across
  36.6 0.7 collective-permute-done.1.next_chip
  37.3 0.1 collective-permute-done.next_core
  37.4 0.5 shard_map.66
  38.0 4.9 %collective-permute-start.3 = (bf16[128,256]{1,0:T(8,128)(2,1)S(1)}, bf16[128,256]{1,0:T(8,128)(2,1)S(1)}, u32[]{:S(2)}, u32[]{:S(2)}) collective-permute-start(bf16[128,256]{1,0:T(8,128)(2,1)S(1)} %get-tuple-element.18.total), channel_id=1, source_target_pairs={{0,64},{16,80},{32,96},{48,112},{64,128},{80,144},{96,160},{112,17... | collective-permute-start | bytes 196616 | tf_op jit(solution)/shard_map/ppermute | solution.py:318
  42.9 1.6 %shard_map.68 = (bf16[1024,256]{1,0:T(8,128)(2,1)S(1)}, f32[1024,128]{1,0:T(8,128)S(1)}) custom-call(bf16[16,200,128]{2,1,0:T(8,128)(2,1)S(1)} %all_to_all.10.received, f32[8,128,256]{2,1,0:T(8,128)S(1)} %get-tuple-element.20.prefixes, f32[8,128,256]{2,1,0:T(8,128)S(1)} %get-tuple-element.21.solved), custom_call_target="tpu_custom_call" | custom-call | flops 8589934592 | bytes 2916352 | tf_op jit(solution)/shard_map/pallas_call | solution.py:263
  44.5 0.0 collective-permute-done.3.earlier
  44.5 0.1 shard_map.67
  44.7 16.1 %collective-permute-start.5 = (bf16[128,256]{1,0:T(8,128)(2,1)S(1)}, bf16[128,256]{1,0:T(8,128)(2,1)S(1)}, u32[]{:S(2)}, u32[]{:S(2)}) collective-permute-start(bf16[128,256]{1,0:T(8,128)(2,1)S(1)} %shard_map.67), channel_id=1, source_target_pairs={{0,288},{16,304},{32,256},{48,272},{64,352},{80,368},{96,320},{112... | collective-permute-start | bytes 196616 | tf_op jit(solution)/shard_map/ppermute | solution.py:323
  60.8 4.3 %collective-permute-start.4 = (bf16[128,256]{1,0:T(8,128)(2,1)S(1)}, bf16[128,256]{1,0:T(8,128)(2,1)S(1)}, u32[]{:S(2)}, u32[]{:S(2)}) collective-permute-start(bf16[128,256]{1,0:T(8,128)(2,1)S(1)} %shard_map.67), channel_id=1, source_target_pairs={{0,128},{16,144},{32,160},{48,176},{64,192},{80,208},{96,224},{112... | collective-permute-start | bytes 196616 | tf_op jit(solution)/shard_map/ppermute | solution.py:318
  65.0 1.3 %collective-permute-start.6 = (bf16[128,128]{1,0:T(8,128)(2,1)S(1)}, bf16[128,128]{1,0:T(8,128)(2,1)S(1)}, u32[]{:S(2)}, u32[]{:S(2)}) collective-permute-start(bf16[128,128]{1,0:T(8,128)(2,1)S(1)} %slice.4), channel_id=1, source_target_pairs={{0,384},{16,400},{32,416},{48,432},{64,448},{80,464},{96,480},{112... | collective-permute-start | bytes 98312 | tf_op jit(solution)/shard_map/ppermute | solution.py:318
  66.3 0.6 shard_map.69
  67.0 1.9 %collective-permute-done.6.farthest = bf16[128,128]{1,0:T(8,128)(2,1)S(1)} collective-permute-done((bf16[128,128]{1,0:T(8,128)(2,1)S(1)}, bf16[128,128]{1,0:T(8,128)(2,1)S(1)}, u32[]{:S(2)}, u32[]{:S(2)}) %collective-permute-start.6) | collective-permute-done | bytes 32800 | tf_op jit(solution)/shard_map/ppermute | solution.py:318
  68.9 0.0 collective-permute-done.5.far
  68.9 0.0 collective-permute-done.4.near
  68.9 0.7 shard_map.70
  69.6 10.6 %all_to_all.11.received = bf16[16,64,128]{2,1,0:T(8,128)(2,1)S(1)} all-to-all(bf16[16,64,128]{2,1,0:T(8,128)(2,1)S(1)} %bitcast.5), channel_id=1, replica_groups=mesh['seq'=32,'head'=16] {'head'}, dimensions={0} | all-to-all | bytes 524288 | tf_op jit(solution)/shard_map/all_to_all | solution.py:344
  80.2 1.0 %shard_map.71 = bf16[64,16,128]{2,1,0:T(8,128)(2,1)} custom-call(bf16[16,64,128]{2,1,0:T(8,128)(2,1)S(1)} %all_to_all.11.received), custom_call_target="tpu_custom_call" | custom-call | bytes 262144 | tf_op jit(solution)/shard_map/pallas_call | solution.py:263
  (1 shorter events, 0.0 us)
Async XLA Ops:
  25.4 11.2 %collective-permute-start.2 = (bf16[128,256]{1,0:T(8,128)(2,1)S(1)}, bf16[128,256]{1,0:T(8,128)(2,1)S(1)}, u32[]{:S(2)}, u32[]{:S(2)}) collective-permute-start(bf16[128,256]{1,0:T(8,128)(2,1)S(1)} %get-tuple-element.17.own), channel_id=1, source_target_pairs={{0,48},{16,32},{32,16},{48,0},{64,112},{80,96},{96,80},{112,64},{1... | collective-permute-start | bytes 196616 | tf_op jit(solution)/shard_map/ppermute | solution.py:301
  32.3 5.0 %collective-permute-start.1 = (bf16[128,256]{1,0:T(8,128)(2,1)S(1)}, bf16[128,256]{1,0:T(8,128)(2,1)S(1)}, u32[]{:S(2)}, u32[]{:S(2)}) collective-permute-start(bf16[128,256]{1,0:T(8,128)(2,1)S(1)} %get-tuple-element.17.own), channel_id=1, source_target_pairs={{0,32},{16,48},{32,0},{48,16},{64,96},{80,112},{96,64},{112,80},{1... | collective-permute-start | bytes 196616 | tf_op jit(solution)/shard_map/ppermute | solution.py:301
  34.3 3.2 %collective-permute-start = (bf16[128,256]{1,0:T(8,128)(2,1)S(1)}, bf16[128,256]{1,0:T(8,128)(2,1)S(1)}, u32[]{:S(2)}, u32[]{:S(2)}) collective-permute-start(bf16[128,256]{1,0:T(8,128)(2,1)S(1)} %get-tuple-element.17.own), channel_id=1, source_target_pairs={{0,16},{16,0},{32,48},{48,32},{64,80},{80,64},{96,112},{112,96},{1... | collective-permute-start | bytes 196616 | tf_op jit(solution)/shard_map/ppermute | solution.py:301
  38.0 6.6 %collective-permute-start.3 = (bf16[128,256]{1,0:T(8,128)(2,1)S(1)}, bf16[128,256]{1,0:T(8,128)(2,1)S(1)}, u32[]{:S(2)}, u32[]{:S(2)}) collective-permute-start(bf16[128,256]{1,0:T(8,128)(2,1)S(1)} %get-tuple-element.18.total), channel_id=1, source_target_pairs={{0,64},{16,80},{32,96},{48,112},{64,128},{80,144},{96,160},{112,17... | collective-permute-start | bytes 196616 | tf_op jit(solution)/shard_map/ppermute | solution.py:318
  44.7 24.2 %collective-permute-start.5 = (bf16[128,256]{1,0:T(8,128)(2,1)S(1)}, bf16[128,256]{1,0:T(8,128)(2,1)S(1)}, u32[]{:S(2)}, u32[]{:S(2)}) collective-permute-start(bf16[128,256]{1,0:T(8,128)(2,1)S(1)} %shard_map.67), channel_id=1, source_target_pairs={{0,288},{16,304},{32,256},{48,272},{64,352},{80,368},{96,320},{112... | collective-permute-start | bytes 196616 | tf_op jit(solution)/shard_map/ppermute | solution.py:323
  60.8 8.1 %collective-permute-start.4 = (bf16[128,256]{1,0:T(8,128)(2,1)S(1)}, bf16[128,256]{1,0:T(8,128)(2,1)S(1)}, u32[]{:S(2)}, u32[]{:S(2)}) collective-permute-start(bf16[128,256]{1,0:T(8,128)(2,1)S(1)} %shard_map.67), channel_id=1, source_target_pairs={{0,128},{16,144},{32,160},{48,176},{64,192},{80,208},{96,224},{112... | collective-permute-start | bytes 196616 | tf_op jit(solution)/shard_map/ppermute | solution.py:318
  65.0 3.9 %collective-permute-start.6 = (bf16[128,128]{1,0:T(8,128)(2,1)S(1)}, bf16[128,128]{1,0:T(8,128)(2,1)S(1)}, u32[]{:S(2)}, u32[]{:S(2)}) collective-permute-start(bf16[128,128]{1,0:T(8,128)(2,1)S(1)} %slice.4), channel_id=1, source_target_pairs={{0,384},{16,400},{32,416},{48,432},{64,448},{80,464},{96,480},{112... | collective-permute-start | bytes 98312 | tf_op jit(solution)/shard_map/ppermute | solution.py:318
